TPU v7x, 256 devices: a whole 4x4x8 slice. The times are simulated.
256 devices in a mesh: row: 16 (over x_lo, y, core), col: 16 (over x_hi, z).
Axes of the slice: x: 4 (x_hi: 2, x_lo: 2; x = x_hi * 2 + x_lo), y: 4, z: 8, core: 2. Of those that a mesh axis runs over, the one named last changes fastest.
Arguments:
- queries: bfloat16 [4096, 8192], P('row', 'col'), may hold values from -96 to 96
- keys: bfloat16 [4096, 1024], P('row'), may hold values from -4.05 to 4.05
- values: bfloat16 [4096, 1024], P('row'), may hold values from -4 to 4
- grad_attn: bfloat16 [4096, 8192], P('row', 'col'), may hold values from -12 to 12
- segment_ids: int32 [4096], replicated, may hold values from 0 to 3, as said below
- q_weight: bfloat16 [8192, 8192], P('row', 'col'), may hold values from -0.0625 to 0.0625
Outputs:
- input_grad: bfloat16 [4096, 8192], P('row', 'col')
- key_grad: bfloat16 [4096, 1024], P('row')
- value_grad: bfloat16 [4096, 1024], P('row')
Inputs may be any that keep to these rules, and one draw needn't show every extreme that they name: `segment_ids`: document numbers never fall along the sequence; a document holds 1 to 2048 positions; the last document holds exactly the last 2048 positions.
All inputs are finite; a program needn't handle non-finite values.
Results may differ from a plain program's by a relative error of at most 0.015.
Values may be sent and summed in bfloat16 or wider, within the bound.
A program may use at most 64 MiB of HBM per device.

v0:
```python
import math

import jax
import jax.numpy as jnp
from jax import lax
from jax.sharding import PartitionSpec as P

H = 64
KVH = 8
HD = 128


NEG_FILL = -1e30


def shortened(array):

    def short(part):
        return part.astype(jnp.bfloat16) if part.dtype == jnp.float32 else part

    return jax.tree.map(short, array)


def shifted(block, axis, distance):
    devices = range(lax.axis_size(axis))
    route = [((i - distance) % len(devices), i) for i in devices]
    return lax.ppermute(block, axis, route)


def local(queries, keys, values, grad_attn, segment_ids, q_weight):
    inv_root = 1.0 / math.sqrt(HD)
    rows_here = queries.shape[0]
    row_count = lax.axis_size("row")
    heads_here = queries.shape[1] // HD
    group_size = H // KVH
    kv_here = max(1, heads_here // group_size)
    per_kv = heads_here // kv_here
    kv_width = kv_here * HD
    half_rows = rows_here // 2
    total_rows = row_count * rows_here
    row_index = lax.axis_index("row")
    col_index = lax.axis_index("col")
    kv_first = col_index * heads_here // group_size
    key_mine = lax.dynamic_slice_in_dim(keys, kv_first * HD, kv_width, 1)
    value_mine = lax.dynamic_slice_in_dim(values, kv_first * HD, kv_width, 1)
    query_local = queries.reshape(rows_here, kv_here, per_kv, HD)
    grad_local = grad_attn.reshape(rows_here, kv_here, per_kv, HD)

    def sequence_place(array_rows):
        shard_of = array_rows // rows_here
        local_of = array_rows % rows_here
        return jnp.where(
            local_of < half_rows,
            shard_of * half_rows + local_of,
            total_rows - (shard_of + 1) * half_rows + local_of - half_rows,
        )

    query_places = sequence_place(row_index * rows_here + jnp.arange(rows_here, dtype=jnp.int32))
    query_segs = jnp.take(segment_ids, query_places)

    def block_mask(first_row, key_count):
        key_places = sequence_place(first_row + jnp.arange(key_count, dtype=jnp.int32))
        key_segs = jnp.take(segment_ids, key_places)
        return (key_places[None, :] <= query_places[:, None]) & (
            key_segs[None, :] == query_segs[:, None]
        )

    def scores_and_grads(key_blk, value_blk):
        key_count = key_blk.shape[0]
        key_split = key_blk.reshape(key_count, kv_here, HD)
        value_split = value_blk.reshape(key_count, kv_here, HD)
        scores = (
            jnp.einsum("qgph,kgh->gpqk", query_local, key_split, preferred_element_type=jnp.float32)
            * inv_root
        )
        grad_prob = jnp.einsum(
            "qgph,kgh->gpqk", grad_local, value_split, preferred_element_type=jnp.float32
        )
        return (key_split, scores, grad_prob)

    def stats_step(state_now, pieces, first_row):
        row_top, row_sum, row_dot = state_now
        key_blk, value_blk = pieces
        allowed = block_mask(first_row, key_blk.shape[0])
        key_split, scores, grad_prob = scores_and_grads(key_blk, value_blk)
        masked = jnp.where(allowed, scores, NEG_FILL)
        new_top = jnp.maximum(row_top, jnp.max(masked, axis=-1))
        expo = jnp.where(allowed, jnp.exp(masked - new_top[..., None]), 0.0)
        factor = jnp.exp(row_top - new_top)
        new_sum = row_sum * factor + jnp.sum(expo, axis=-1)
        new_dot = row_dot * factor + jnp.sum(expo * grad_prob, axis=-1)
        return (new_top, new_sum, new_dot)

    def backward_block(key_blk, value_blk, first_row, row_lse, prob_dot):
        key_count = key_blk.shape[0]
        allowed = block_mask(first_row, key_count)
        key_split, scores, grad_prob = scores_and_grads(key_blk, value_blk)
        softmax_w = jnp.exp(jnp.where(allowed, scores - row_lse[..., None], NEG_FILL))
        softmax_w = jnp.where(allowed, softmax_w, 0.0)
        dscore = (softmax_w * (grad_prob - prob_dot[..., None])).astype(jnp.bfloat16)
        soft_low = softmax_w.astype(jnp.bfloat16)
        query_part = jnp.einsum(
            "gpqk,kgh->qgph", dscore, key_split, preferred_element_type=jnp.float32
        )
        key_part = jnp.einsum(
            "gpqk,qgph->kgh", dscore, query_local, preferred_element_type=jnp.float32
        )
        value_part = jnp.einsum(
            "gpqk,qgph->kgh", soft_low, grad_local, preferred_element_type=jnp.float32
        )
        return (
            query_part,
            key_part.reshape(key_count, kv_width),
            value_part.reshape(key_count, kv_width),
        )

    stat_shape = (kv_here, per_kv, rows_here)
    stat_init = (
        jnp.full(stat_shape, NEG_FILL, jnp.float32),
        jnp.zeros(stat_shape, jnp.float32),
        jnp.zeros(stat_shape, jnp.float32),
    )
    query_zero = jnp.zeros((rows_here, kv_here, per_kv, HD), jnp.float32)

    def pass_keys(pair):
        return jax.tree.map(
            lambda part, own: part.astype(own.dtype), shifted(shortened(pair), "row", 1), pair
        )

    def stats_turn(cycle_step, state_now):
        key_blk, value_blk, stats_now = state_now
        owner_row = (row_index - cycle_step) % row_count
        stats_now = stats_step(stats_now, (key_blk, value_blk), owner_row * rows_here)
        key_blk, value_blk = pass_keys((key_blk, value_blk))
        return (key_blk, value_blk, stats_now)

    stats_loop = lax.fori_loop(0, row_count, stats_turn, (key_mine, value_mine, stat_init))
    row_top, row_sum, row_dot = stats_loop[2]
    row_lse = row_top + jnp.log(row_sum)
    prob_dot = row_dot / row_sum

    def grad_turn(cycle_step, state_now):
        key_blk, value_blk, key_acc, value_acc, query_acc = state_now
        owner_row = (row_index - cycle_step) % row_count
        query_part, key_part, value_part = backward_block(
            key_blk, value_blk, owner_row * rows_here, row_lse, prob_dot
        )
        key_blk, value_blk = pass_keys((key_blk, value_blk))
        key_acc, value_acc = shifted((key_acc + key_part, value_acc + value_part), "row", 1)
        return (key_blk, value_blk, key_acc, value_acc, query_acc + query_part)

    zero_grad = jnp.zeros((rows_here, kv_width), jnp.float32)
    grad_loop = lax.fori_loop(
        0, row_count, grad_turn, (key_mine, value_mine, zero_grad, zero_grad, query_zero)
    )
    key_mine_grad = grad_loop[2]
    value_mine_grad = grad_loop[3]
    query_acc = grad_loop[4]
    wide_zero = jnp.zeros((rows_here, KVH * HD), jnp.float32)
    key_wide = lax.dynamic_update_slice_in_dim(wide_zero, key_mine_grad, kv_first * HD, 1)
    value_wide = lax.dynamic_update_slice_in_dim(wide_zero, value_mine_grad, kv_first * HD, 1)
    key_sum, value_sum = (
        lax.psum(key_wide.astype(jnp.bfloat16), "col").astype(jnp.float32),
        lax.psum(value_wide.astype(jnp.bfloat16), "col").astype(jnp.float32),
    )
    key_grad = (key_sum * inv_root).astype(jnp.bfloat16)
    value_grad = value_sum.astype(jnp.bfloat16)
    query_grad = (query_acc * inv_root).reshape(rows_here, heads_here * HD).astype(jnp.bfloat16)
    query_wide = lax.all_gather(query_grad, "col", axis=1, tiled=True)
    input_sum = jnp.dot(
        query_wide,
        lax.all_gather(q_weight, "row", axis=0, tiled=True),
        preferred_element_type=jnp.float32,
    )
    return (input_sum.astype(jnp.bfloat16), key_grad, value_grad)


def solution(mesh):
    placed = (
        P("row", "col"),
        P("row", None),
        P("row", None),
        P("row", "col"),
        P(),
        P("row", "col"),
    )
    return jax.shard_map(
        local,
        mesh=mesh,
        in_specs=placed,
        out_specs=(P("row", "col"), P("row", None), P("row", None)),
        check_vma=False,
    )
```

profile of v0, /device:TPU:1, one launch (start us, length us, event | category | flops | bytes accessed | tf_op | source)
XLA Modules:
  0.0 630.6 jit_solution(16788450805528187902)
XLA Ops:
  12.8 101.8 %while.50 = (s32[]{:T(128)}, bf16[256,128]{1,0:T(8,128)(2,1)S(1)}, bf16[256,128]{1,0:T(8,128)(2,1)S(1)}, f32[1,4,256]{2,1,0:T(4,128)S(1)}, f32[1,4,256]{2,1,0:T(...) while((s32[]{:T(128)}, bf16[256,128]{1,0:T(8,128)(2,1)S(1)}, ...), condition=%wide.region_4.6_spmd.clone, body=%wide.region_0.5_spmd.clone.sunk | while | flops 137068816 | bytes 4941193 | solution.py:137
  12.8 2.8 collective-permute-start
  33.3 3.1 collective-permute-done
  39.8 3.1 collective-permute-done
  46.3 3.1 collective-permute-done
  52.8 3.1 collective-permute-done
  59.3 3.1 collective-permute-done
  65.8 3.1 collective-permute-done
  72.3 3.1 collective-permute-done
  78.8 3.1 collective-permute-done
  85.4 3.1 collective-permute-done
  91.9 3.1 collective-permute-done
  98.4 3.1 collective-permute-done
  104.9 3.1 collective-permute-done
  111.4 3.1 collective-permute-done
  114.6 181.8 %while.51 = (s32[]{:T(128)}, bf16[256,128]{1,0:T(8,128)(2,1)S(1)}, bf16[256,128]{1,0:T(8,128)(2,1)S(1)}, f32[256,128]{1,0:T(8,128)S(1)}, f32[256,128]{1,0:T(8,12...) while((s32[]{:T(128)}, bf16[256,128]{1,0:T(8,128)(2,1)S(1)}, ...), condition=%wide.region_6.8_spmd.clone, body=%wide.region_5.7_spmd.clone.sunk | while | flops 338191616 | bytes 9528808 | solution.py:153
  118.1 2.9 collective-permute-start.4
  121.9 2.7 collective-permute-done.4
  130.7 2.6 collective-permute-start.4
  143.1 2.6 collective-permute-start.4
  299.3 150.9 %all-reduce.3.cloned.1.call-done = (bf16[256,1024]{1,0:T(8,128)(2,1)}, bf16[256,1024]{1,0:T(8,128)(2,1)}) async-done(((bf16[256,1024]{1,0:T(8,128)(2,1)}, bf16[256,1024]{1,0:T(8,128)(2,1)}), (bf16[256,1024]{1,0:T(8,128)(2,1)}, bf16[256,1024]{1,0:T(8,128)(2,1)})) %all-reduce.3.cloned.1.call-update) | async-done | bytes 1048592 | tf_op jit(solution)/shard_map/psum | solution.py:163
  452.2 106.5 %all-gather.3.cloned.1.call-done = bf16[256,8192]{0,1:T(8,128)(2,1)} async-done(((bf16[256,512]{0,1:T(8,128)(2,1)}), bf16[256,8192]{0,1:T(8,128)(2,1)}) %all-gather.3.cloned.1.call-update) | async-done | bytes 4194320 | tf_op jit(solution)/shard_map/all_gather | solution.py:169
  558.7 56.9 %all-gather.5.cloned.1.call-done = bf16[8192,512]{1,0:T(8,128)(2,1)} async-done(((bf16[512,512]{1,0:T(8,128)(2,1)}), bf16[8192,512]{1,0:T(8,128)(2,1)}) %all-gather.5.cloned.1.call-update) | async-done | bytes 8388624 | tf_op jit(solution)/shard_map/all_gather | solution.py:172
  615.6 7.7 %convolution_convert_fusion = bf16[256,512]{1,0:T(8,128)(2,1)} fusion(bf16[256,8192]{0,1:T(8,128)(2,1)} %all-gather.3.cloned.1.call-done, bf16[8192,512]{1,0:T(8,128)(2,1)} %all-gather.5.cloned.1.call-done), kind=kOutput, calls=%fused_computation.81 | convolution fusion | flops 2147614720 | bytes 12845056 | tf_op jit(solution)/shard_map/dot_general | solution.py:170
  (644 shorter events, 237.7 us)
Async XLA Ops:
  7.2 443.1 %all-reduce.3.cloned.1.call-start = ((), (), s32[]{:S(2)}) async-start(), calls=%async_computation.2 | async-start | bytes 2097152 | tf_op jit(solution)/shard_map/psum | solution.py:163
  114.7 7.2 %collective-permute-start.2 = (bf16[256,128]{1,0:T(8,128)(2,1)S(1)}, bf16[256,128]{1,0:T(8,128)(2,1)S(1)}, u32[]{:S(2)}, u32[]{:S(2)}) collective-permute-start(bf16[256,128]{1,0:T(8,128)(2,1)S(1)} %copy.44), channel_id=1, source_target_pairs={{240,0},{0,16},{16,32},{32,48},{48,64},{64,80},{80,96},{96,112},{1... | collective-permute-start | bytes 196616 | tf_op jit(solution)/shard_map/while/body/eval_jaxpr/ppermute | solution.py:27
  114.8 7.1 %collective-permute-start.3 = (bf16[256,128]{1,0:T(8,128)(2,1)S(1)}, bf16[256,128]{1,0:T(8,128)(2,1)S(1)}, u32[]{:S(2)}, u32[]{:S(2)}) collective-permute-start(bf16[256,128]{1,0:T(8,128)(2,1)S(1)} %copy.45), channel_id=1, source_target_pairs={{240,0},{0,16},{16,32},{32,48},{48,64},{64,80},{80,96},{96,112},{1... | collective-permute-start | bytes 196616 | tf_op jit(solution)/shard_map/while/body/eval_jaxpr/ppermute | solution.py:27
  118.1 6.6 %collective-permute-start.4 = (f32[256,128]{1,0:T(8,128)S(1)}, f32[256,128]{1,0:T(8,128)S(1)}, u32[]{:S(2)}, u32[]{:S(2)}) collective-permute-start(f32[256,128]{1,0:T(8,128)S(1)} %fusion.77), channel_id=1, source_target_pairs={{240,0},{0,16},{16,32},{32,48},{48,64},{64,80},{80,96},{96,112},{1... | collective-permute-start | bytes 393224 | tf_op jit(solution)/shard_map/while/body/eval_jaxpr/ppermute | solution.py:27
  125.1 9.9 %collective-permute-start.2 = (bf16[256,128]{1,0:T(8,128)(2,1)S(1)}, bf16[256,128]{1,0:T(8,128)(2,1)S(1)}, u32[]{:S(2)}, u32[]{:S(2)}) collective-permute-start(bf16[256,128]{1,0:T(8,128)(2,1)S(1)} %copy.44), channel_id=1, source_target_pairs={{240,0},{0,16},{16,32},{32,48},{48,64},{64,80},{80,96},{96,112},{1... | collective-permute-start | bytes 196616 | tf_op jit(solution)/shard_map/while/body/eval_jaxpr/ppermute | solution.py:27
  126.8 8.2 %collective-permute-start.3 = (bf16[256,128]{1,0:T(8,128)(2,1)S(1)}, bf16[256,128]{1,0:T(8,128)(2,1)S(1)}, u32[]{:S(2)}, u32[]{:S(2)}) collective-permute-start(bf16[256,128]{1,0:T(8,128)(2,1)S(1)} %copy.45), channel_id=1, source_target_pairs={{240,0},{0,16},{16,32},{32,48},{48,64},{64,80},{80,96},{96,112},{1... | collective-permute-start | bytes 196616 | tf_op jit(solution)/shard_map/while/body/eval_jaxpr/ppermute | solution.py:27
  136.6 10.0 %collective-permute-start.2 = (bf16[256,128]{1,0:T(8,128)(2,1)S(1)}, bf16[256,128]{1,0:T(8,128)(2,1)S(1)}, u32[]{:S(2)}, u32[]{:S(2)}) collective-permute-start(bf16[256,128]{1,0:T(8,128)(2,1)S(1)} %copy.44), channel_id=1, source_target_pairs={{240,0},{0,16},{16,32},{32,48},{48,64},{64,80},{80,96},{96,112},{1... | collective-permute-start | bytes 196616 | tf_op jit(solution)/shard_map/while/body/eval_jaxpr/ppermute | solution.py:27
  139.1 7.5 %collective-permute-start.3 = (bf16[256,128]{1,0:T(8,128)(2,1)S(1)}, bf16[256,128]{1,0:T(8,128)(2,1)S(1)}, u32[]{:S(2)}, u32[]{:S(2)}) collective-permute-start(bf16[256,128]{1,0:T(8,128)(2,1)S(1)} %copy.45), channel_id=1, source_target_pairs={{240,0},{0,16},{16,32},{32,48},{48,64},{64,80},{80,96},{96,112},{1... | collective-permute-start | bytes 196616 | tf_op jit(solution)/shard_map/while/body/eval_jaxpr/ppermute | solution.py:27
  149.0 9.0 %collective-permute-start.2 = (bf16[256,128]{1,0:T(8,128)(2,1)S(1)}, bf16[256,128]{1,0:T(8,128)(2,1)S(1)}, u32[]{:S(2)}, u32[]{:S(2)}) collective-permute-start(bf16[256,128]{1,0:T(8,128)(2,1)S(1)} %copy.44), channel_id=1, source_target_pairs={{240,0},{0,16},{16,32},{32,48},{48,64},{64,80},{80,96},{96,112},{1... | collective-permute-start | bytes 196616 | tf_op jit(solution)/shard_map/while/body/eval_jaxpr/ppermute | solution.py:27
  151.5 6.5 %collective-permute-start.3 = (bf16[256,128]{1,0:T(8,128)(2,1)S(1)}, bf16[256,128]{1,0:T(8,128)(2,1)S(1)}, u32[]{:S(2)}, u32[]{:S(2)}) collective-permute-start(bf16[256,128]{1,0:T(8,128)(2,1)S(1)} %copy.45), channel_id=1, source_target_pairs={{240,0},{0,16},{16,32},{32,48},{48,64},{64,80},{80,96},{96,112},{1... | collective-permute-start | bytes 196616 | tf_op jit(solution)/shard_map/while/body/eval_jaxpr/ppermute | solution.py:27
  160.4 8.9 %collective-permute-start.2 = (bf16[256,128]{1,0:T(8,128)(2,1)S(1)}, bf16[256,128]{1,0:T(8,128)(2,1)S(1)}, u32[]{:S(2)}, u32[]{:S(2)}) collective-permute-start(bf16[256,128]{1,0:T(8,128)(2,1)S(1)} %copy.44), channel_id=1, source_target_pairs={{240,0},{0,16},{16,32},{32,48},{48,64},{64,80},{80,96},{96,112},{1... | collective-permute-start | bytes 196616 | tf_op jit(solution)/shard_map/while/body/eval_jaxpr/ppermute | solution.py:27
  171.7 8.9 %collective-permute-start.2 = (bf16[256,128]{1,0:T(8,128)(2,1)S(1)}, bf16[256,128]{1,0:T(8,128)(2,1)S(1)}, u32[]{:S(2)}, u32[]{:S(2)}) collective-permute-start(bf16[256,128]{1,0:T(8,128)(2,1)S(1)} %copy.44), channel_id=1, source_target_pairs={{240,0},{0,16},{16,32},{32,48},{48,64},{64,80},{80,96},{96,112},{1... | collective-permute-start | bytes 196616 | tf_op jit(solution)/shard_map/while/body/eval_jaxpr/ppermute | solution.py:27
  183.1 8.9 %collective-permute-start.2 = (bf16[256,128]{1,0:T(8,128)(2,1)S(1)}, bf16[256,128]{1,0:T(8,128)(2,1)S(1)}, u32[]{:S(2)}, u32[]{:S(2)}) collective-permute-start(bf16[256,128]{1,0:T(8,128)(2,1)S(1)} %copy.44), channel_id=1, source_target_pairs={{240,0},{0,16},{16,32},{32,48},{48,64},{64,80},{80,96},{96,112},{1... | collective-permute-start | bytes 196616 | tf_op jit(solution)/shard_map/while/body/eval_jaxpr/ppermute | solution.py:27
  194.4 8.9 %collective-permute-start.2 = (bf16[256,128]{1,0:T(8,128)(2,1)S(1)}, bf16[256,128]{1,0:T(8,128)(2,1)S(1)}, u32[]{:S(2)}, u32[]{:S(2)}) collective-permute-start(bf16[256,128]{1,0:T(8,128)(2,1)S(1)} %copy.44), channel_id=1, source_target_pairs={{240,0},{0,16},{16,32},{32,48},{48,64},{64,80},{80,96},{96,112},{1... | collective-permute-start | bytes 196616 | tf_op jit(solution)/shard_map/while/body/eval_jaxpr/ppermute | solution.py:27
  205.7 8.9 %collective-permute-start.2 = (bf16[256,128]{1,0:T(8,128)(2,1)S(1)}, bf16[256,128]{1,0:T(8,128)(2,1)S(1)}, u32[]{:S(2)}, u32[]{:S(2)}) collective-permute-start(bf16[256,128]{1,0:T(8,128)(2,1)S(1)} %copy.44), channel_id=1, source_target_pairs={{240,0},{0,16},{16,32},{32,48},{48,64},{64,80},{80,96},{96,112},{1... | collective-permute-start | bytes 196616 | tf_op jit(solution)/shard_map/while/body/eval_jaxpr/ppermute | solution.py:27
  217.1 8.9 %collective-permute-start.2 = (bf16[256,128]{1,0:T(8,128)(2,1)S(1)}, bf16[256,128]{1,0:T(8,128)(2,1)S(1)}, u32[]{:S(2)}, u32[]{:S(2)}) collective-permute-start(bf16[256,128]{1,0:T(8,128)(2,1)S(1)} %copy.44), channel_id=1, source_target_pairs={{240,0},{0,16},{16,32},{32,48},{48,64},{64,80},{80,96},{96,112},{1... | collective-permute-start | bytes 196616 | tf_op jit(solution)/shard_map/while/body/eval_jaxpr/ppermute | solution.py:27
  228.4 8.9 %collective-permute-start.2 = (bf16[256,128]{1,0:T(8,128)(2,1)S(1)}, bf16[256,128]{1,0:T(8,128)(2,1)S(1)}, u32[]{:S(2)}, u32[]{:S(2)}) collective-permute-start(bf16[256,128]{1,0:T(8,128)(2,1)S(1)} %copy.44), channel_id=1, source_target_pairs={{240,0},{0,16},{16,32},{32,48},{48,64},{64,80},{80,96},{96,112},{1... | collective-permute-start | bytes 196616 | tf_op jit(solution)/shard_map/while/body/eval_jaxpr/ppermute | solution.py:27
  239.8 8.9 %collective-permute-start.2 = (bf16[256,128]{1,0:T(8,128)(2,1)S(1)}, bf16[256,128]{1,0:T(8,128)(2,1)S(1)}, u32[]{:S(2)}, u32[]{:S(2)}) collective-permute-start(bf16[256,128]{1,0:T(8,128)(2,1)S(1)} %copy.44), channel_id=1, source_target_pairs={{240,0},{0,16},{16,32},{32,48},{48,64},{64,80},{80,96},{96,112},{1... | collective-permute-start | bytes 196616 | tf_op jit(solution)/shard_map/while/body/eval_jaxpr/ppermute | solution.py:27
  251.1 8.9 %collective-permute-start.2 = (bf16[256,128]{1,0:T(8,128)(2,1)S(1)}, bf16[256,128]{1,0:T(8,128)(2,1)S(1)}, u32[]{:S(2)}, u32[]{:S(2)}) collective-permute-start(bf16[256,128]{1,0:T(8,128)(2,1)S(1)} %copy.44), channel_id=1, source_target_pairs={{240,0},{0,16},{16,32},{32,48},{48,64},{64,80},{80,96},{96,112},{1... | collective-permute-start | bytes 196616 | tf_op jit(solution)/shard_map/while/body/eval_jaxpr/ppermute | solution.py:27
  262.4 8.9 %collective-permute-start.2 = (bf16[256,128]{1,0:T(8,128)(2,1)S(1)}, bf16[256,128]{1,0:T(8,128)(2,1)S(1)}, u32[]{:S(2)}, u32[]{:S(2)}) collective-permute-start(bf16[256,128]{1,0:T(8,128)(2,1)S(1)} %copy.44), channel_id=1, source_target_pairs={{240,0},{0,16},{16,32},{32,48},{48,64},{64,80},{80,96},{96,112},{1... | collective-permute-start | bytes 196616 | tf_op jit(solution)/shard_map/while/body/eval_jaxpr/ppermute | solution.py:27
  273.8 8.9 %collective-permute-start.2 = (bf16[256,128]{1,0:T(8,128)(2,1)S(1)}, bf16[256,128]{1,0:T(8,128)(2,1)S(1)}, u32[]{:S(2)}, u32[]{:S(2)}) collective-permute-start(bf16[256,128]{1,0:T(8,128)(2,1)S(1)} %copy.44), channel_id=1, source_target_pairs={{240,0},{0,16},{16,32},{32,48},{48,64},{64,80},{80,96},{96,112},{1... | collective-permute-start | bytes 196616 | tf_op jit(solution)/shard_map/while/body/eval_jaxpr/ppermute | solution.py:27
  285.1 8.9 %collective-permute-start.2 = (bf16[256,128]{1,0:T(8,128)(2,1)S(1)}, bf16[256,128]{1,0:T(8,128)(2,1)S(1)}, u32[]{:S(2)}, u32[]{:S(2)}) collective-permute-start(bf16[256,128]{1,0:T(8,128)(2,1)S(1)} %copy.44), channel_id=1, source_target_pairs={{240,0},{0,16},{16,32},{32,48},{48,64},{64,80},{80,96},{96,112},{1... | collective-permute-start | bytes 196616 | tf_op jit(solution)/shard_map/while/body/eval_jaxpr/ppermute | solution.py:27
  297.5 261.2 %all-gather.3.cloned.1.call-start = ((), (), s32[]{:S(2)}) async-start(), calls=%async_computation | async-start | bytes 4456448 | tf_op jit(solution)/shard_map/all_gather | solution.py:169
  298.6 317.0 %all-gather.5.cloned.1.call-start = ((), (), s32[]{:S(2)}) async-start(), calls=%async_computation.1 | async-start | bytes 8912896 | tf_op jit(solution)/shard_map/all_gather | solution.py:172
  (78 other events, 559.2 us)
Sparse Core Ops, SparseCore 0:
  297.7 152.5 all-reduce.2
  453.8 104.9 all-gather.2
  560.7 54.8 all-gather.4
where the time goes:
time: 634 us; the launch traced here: 631 us
  waiting for transfers between devices  396 us (62%)
  starting transfers between devices  87.1 us (14%)
  local copies, waits for them, and re-layouts  70.5 us (11%)
  matrix products  46.6 us (7%)
  between operations  13.9 us (2%)
  other arithmetic  13.1 us (2%)
    psum x1, waiting for transfers between devices, local(): lax.psum(key_wide.astype(jnp.bfloat16), 'col').astype(jnp.float32)  151 us
    all_gather x1, waiting for transfers between devices, local(): query_wide = lax.all_gather(query_grad, 'col', axis=1, tiled=True)  107 us
    ppermute x96, starting transfers between devices, shifted(): return lax.ppermute(block, axis, route)  87 us
    ppermute x96, waiting for transfers between devices, shifted(): return lax.ppermute(block, axis, route)  81.1 us
    gather x32, local copies, waits for them, and re-layouts, block_mask(): key_segs = jnp.take(segment_ids, key_places)  62.7 us
    all_gather x1, waiting for transfers between devices, local(): lax.all_gather(q_weight, 'row', axis=0, tiled=True)  56.9 us
  transfers between devices with their start and end apart: 99, of which 63 were waited for; matrix products, arithmetic and copies ran while one was open for 18% of the time, Pallas kernels for 0%

commit v1 on v0

v1 whole, which is shorter than its diff:
```python
import functools
import math

import jax
import jax.numpy as jnp
from jax import lax
from jax.experimental import pallas as pl
from jax.experimental.pallas import tpu as pltpu
from jax.sharding import PartitionSpec as P

H = 64
KVH = 8
HD = 128
TOKENS = 4096
HALF = 128
PER = 4
NEG = -1e30
MESH = pl.DeviceIdType.MESH
INV_ROOT = 1.0 / math.sqrt(HD)
SCALE2 = INV_ROOT * math.log2(math.e)
F32 = jnp.float32
BF16 = jnp.bfloat16


def dot_nt(a, b):
    return lax.dot_general(a, b, (((1,), (1,)), ((), ())), preferred_element_type=F32)


def dot_nn(a, b):
    return lax.dot_general(a, b, (((1,), (0,)), ((), ())), preferred_element_type=F32)


def dot_tn(a, b):
    return lax.dot_general(a, b, (((0,), (0,)), ((), ())), preferred_element_type=F32)


def attention_kernel(
    q_ref, k_hbm, v_hbm, g_ref, seg_ref,
    wide_hbm, kout_ref, vout_ref,
    kvbuf, sbuf, dpbuf, q4, g4, dq4, stat, pbuf, rbuf, ownf, pair_s, pair_r, dqbuf, pieces,
    load_sem, kv_send, kv_recv, fw_send, fw_recv, dkv_send, dkv_recv, pair_sem,
    xq_send, xq_recv, xp_sem, z_send, z_recv, p_send, p_recv, out_sem,
):
    s = lax.axis_index("row")
    j = lax.axis_index("col")
    chip, core = s // 2, s % 2
    xh, z = j // 8, j % 8
    sibling = s + 1 - 2 * core
    partner = (1 - xh) * 8 + z
    right = xh * 8 + (z + 1) % 8
    left = xh * 8 + (z + 7) % 8
    parity = z % 2
    mate = j + 1 - 2 * parity
    head = j // 2

    def remote(src, dst, ssem, rsem, row, col):
        return pltpu.make_async_remote_copy(
            src_ref=src, dst_ref=dst, send_sem=ssem, recv_sem=rsem,
            device_id=(row, col), device_id_type=MESH,
        )

    lanes = pl.ds(pl.multiple_of(head * HD, HD), HD)
    loads = []
    for u in range(2):
        slot = s if u == 0 else 16
        for i, ref in enumerate((k_hbm, v_hbm)):
            loads.append(
                pltpu.make_async_copy(
                    ref.at[pl.ds(u * HALF, HALF), lanes], kvbuf.at[slot, i], load_sem.at[2 * u + i]
                )
            )
    for copy in loads:
        copy.start()

    barrier = pltpu.get_barrier_semaphore()

    def greet(e, carry):
        pl.semaphore_signal(barrier, inc=1, device_id=((s + e) % 16, j), device_id_type=MESH)
        return carry

    lax.fori_loop(1, 16, greet, 0)
    for col in (right, left, partner):
        pl.semaphore_signal(barrier, inc=1, device_id=(s, col), device_id_type=MESH)

    for u in range(2):
        for h in range(PER):
            q4[u, h * HD:(h + 1) * HD, :] = q_ref[u * HALF:(u + 1) * HALF, h * HD:(h + 1) * HD]
            g4[u, h * HD:(h + 1) * HD, :] = g_ref[u * HALF:(u + 1) * HALF, h * HD:(h + 1) * HD]

    seg = seg_ref[...]
    counts = [jnp.sum((seg < v).astype(F32), keepdims=True) for v in (1, 2, 3)]
    lane = lax.broadcasted_iota(jnp.int32, (1, HALF), 1).astype(F32)
    bounds = []
    for u in range(2):
        block = s if u == 0 else 31 - s
        seg_q = seg_ref[pl.ds(block, 1), :]
        start = jnp.where(
            seg_q == 0, 0.0,
            jnp.where(seg_q == 1, counts[0], jnp.where(seg_q == 2, counts[1], counts[2])),
        )
        stat[4 + u, 0:1, 0:HALF] = start
        stat[4 + u, 1:2, 0:HALF] = lane + (block * HALF).astype(F32)
        stat[u] = jnp.full((8, PER * HALF), NEG, F32)

    for copy in loads:
        copy.wait()
    pl.semaphore_wait(barrier, 18)

    def kv_copy(d, chip_to, row_to):
        src = kvbuf.at[jnp.where(chip_to > chip, s, 16)]
        return remote(src, kvbuf.at[s], kv_send.at[d], kv_recv.at[d], row_to, j)

    def kv_out(d):
        chip_to = (chip + d) % 8
        return kv_copy(d, chip_to, chip_to * 2 + core)

    def kv_start(d, carry):
        kv_out(d).start()
        return carry

    own_half = kvbuf.at[jnp.where(core == 0, s, 16)]
    to_sibling = remote(own_half, kvbuf.at[s], kv_send.at[0], kv_recv.at[0], sibling, j)
    lax.fori_loop(1, 8, kv_start, 0)
    to_sibling.start()

    sub = lax.broadcasted_iota(jnp.int32, (HALF, HALF), 0).astype(F32)

    def pass_one(t):
        u = jnp.where(t > s, 1, 0)
        block = jnp.where(t > s, jnp.where(t == 16, 31 - s, 31 - t), t)
        key_place = sub + (block * HALF).astype(F32)
        start = stat[4 + u, 0:1, 0:HALF]
        place = stat[4 + u, 1:2, 0:HALF]
        bias = jnp.where((key_place >= start) & (key_place <= place), 0.0, NEG)
        scores = dot_nt(kvbuf[t, 0], q4[u])
        for h in range(PER):
            part = scores[:, h * HALF:(h + 1) * HALF] * SCALE2 + bias
            sbuf[t, :, h * HALF:(h + 1) * HALF] = part
            top = jnp.max(part.reshape(16, 8, HALF), axis=0)
            stat[u, :, h * HALF:(h + 1) * HALF] = jnp.maximum(
                stat[u, :, h * HALF:(h + 1) * HALF], top
            )
        dpbuf[t] = dot_nt(kvbuf[t, 1], g4[u])

    pass_one(s)
    pass_one(16)

    def forward(d):
        origin = ((chip + 8 - d) % 8) * 2 + core
        return remote(kvbuf.at[origin], kvbuf.at[origin], fw_send.at[d], fw_recv.at[d], sibling, j)

    def arrive(d, carry):
        origin = ((chip + 8 - d) % 8) * 2 + core
        remote(
            kvbuf.at[origin], kvbuf.at[origin], kv_send.at[d], kv_recv.at[d], sibling, j
        ).wait_recv()
        forward(d).start()
        pass_one(origin)
        return carry

    lax.fori_loop(1, 8, arrive, 0)
    remote(
        kvbuf.at[sibling], kvbuf.at[sibling], kv_send.at[0], kv_recv.at[0], sibling, j
    ).wait_recv()
    pass_one(sibling)

    def arrive_two(d, carry):
        origin = ((chip + 8 - d) % 8) * 2 + 1 - core
        remote(
            kvbuf.at[origin], kvbuf.at[origin], fw_send.at[d], fw_recv.at[d], sibling, j
        ).wait_recv()
        pass_one(origin)
        return carry

    lax.fori_loop(1, 8, arrive_two, 0)

    for u in range(2):
        top = jnp.max(stat[u], axis=0, keepdims=True)
        stat[u] = jnp.broadcast_to(top, (8, PER * HALF))
        stat[2 + u] = jnp.zeros((8, PER * HALF), F32)
        stat[6 + u] = jnp.zeros((8, PER * HALF), F32)

    def pass_two(t, carry):
        u = jnp.where(t > s, 1, 0)
        for h in range(PER):
            cols = slice(h * HALF, (h + 1) * HALF)
            top = stat[u, 0:1, cols]
            expo = jnp.exp2(sbuf[t, :, cols] - top)
            sbuf[t, :, cols] = expo
            stat[2 + u, :, cols] += jnp.sum(expo.reshape(16, 8, HALF), axis=0)
            stat[6 + u, :, cols] += jnp.sum((expo * dpbuf[t, :, cols]).reshape(16, 8, HALF), axis=0)
        return carry

    lax.fori_loop(0, 17, pass_two, 0)
    for u in range(2):
        total = jnp.sum(stat[2 + u], axis=0, keepdims=True)
        inverse = 1.0 / total
        delta = jnp.sum(stat[6 + u], axis=0, keepdims=True) * inverse
        stat[2 + u, 0:1, :] = inverse
        stat[6 + u, 0:1, :] = delta
        dq4[u] = jnp.zeros((PER * HALF, HD), F32)

    def dkv_out(t):
        return remote(pbuf.at[t], rbuf.at[s], dkv_send.at[t], dkv_recv.at[s], t, j)

    def pass_three(t, carry):
        u = jnp.where(t > s, 1, 0)
        inverse = stat[2 + u, 0:1, :]
        delta = stat[6 + u, 0:1, :]
        probs = sbuf[t] * inverse
        dscore = (probs * (dpbuf[t] - delta)).astype(BF16)
        key_part = dot_nn(dscore, q4[u])
        value_part = dot_nn(probs.astype(BF16), g4[u])
        dq4[u] += dot_tn(dscore, kvbuf[t, 0])
        mine = (t == s) | (t == 16)

        @pl.when(mine)
        def _():
            ownf[u, 0] = key_part
            ownf[u, 1] = value_part

        @pl.when(jnp.logical_not(mine))
        def _():
            pbuf[t, 0] = key_part.astype(BF16)
            pbuf[t, 1] = value_part.astype(BF16)
            dkv_out(t).start()

        return carry

    def x_copy(u):
        rows = pl.ds(u * HALF, HALF)
        src = dqbuf.at[xh, z, rows]
        return remote(src, src, xq_send.at[u], xq_recv.at[u], s, partner)

    def x_wait(u):
        dst = dqbuf.at[1 - xh, z, pl.ds(u * HALF, HALF)]
        remote(dst, dst, xq_send.at[u], xq_recv.at[u], s, partner).wait_recv()

    def z_copy(way, k, e, u):
        origin = (z + 8 - (k - 1)) % 8 if way == 0 else (z + (k - 1)) % 8
        side = xh if e == 0 else 1 - xh
        src = dqbuf.at[side, origin, pl.ds(u * HALF, HALF)]
        index = ((way * 4 + (k - 1)) * 2 + e) * 2 + u
        return remote(src, src, z_send.at[index], z_recv.at[index], s, right if way == 0 else left)

    def z_wait(way, k, e, u):
        origin = (z + 8 - k) % 8 if way == 0 else (z + k) % 8
        side = xh if e == 0 else 1 - xh
        dst = dqbuf.at[side, origin, pl.ds(u * HALF, HALF)]
        index = ((way * 4 + (k - 1)) * 2 + e) * 2 + u
        remote(dst, dst, z_send.at[index], z_recv.at[index], s, right).wait_recv()

    def hops(way, k, u):
        return k <= 3 or u == way

    def z_turn(k, e):
        for u in (1, 0):
            for way in range(2):
                if hops(way, k, u):
                    z_wait(way, k, e, u)
                    if k < 4 and hops(way, k + 1, u):
                        z_copy(way, k + 1, e, u).start()

    for u, first, last in ((1, s + 1, 17), (0, 0, s + 1)):
        lax.fori_loop(first, last, pass_three, 0)
        for h in range(PER):
            dqbuf[xh, z, u * HALF:(u + 1) * HALF, h * HD:(h + 1) * HD] = (
                dq4[u, h * HD:(h + 1) * HD, :] * INV_ROOT
            ).astype(BF16)
        z_copy(0, 1, 0, u).start()
        z_copy(1, 1, 0, u).start()
        x_copy(u).start()

    def spread(side, origin):
        lanes = pl.ds(pl.multiple_of((side * 8 + origin) * 512, 512), 512)
        return pltpu.make_async_copy(
            dqbuf.at[side, origin], wide_hbm.at[:, lanes], out_sem.at[side, origin]
        )

    z_turn(1, 0)
    for u in (1, 0):
        x_wait(u)
        z_copy(0, 1, 1, u).start()
        z_copy(1, 1, 1, u).start()
    z_turn(2, 0)

    def dkv_wait(r, carry):
        remote(rbuf.at[r], rbuf.at[r], dkv_send.at[r], dkv_recv.at[r], s, right).wait_recv()
        return carry

    lax.fori_loop(0, s, dkv_wait, 0)
    lax.fori_loop(s + 1, 16, dkv_wait, 0)

    def add_to(u):
        def add(r, carry):
            for i in range(2):
                ownf[u, i] += rbuf[r, i].astype(F32)
            return carry
        return add

    lax.fori_loop(s + 1, 16, add_to(0), 0)
    lax.fori_loop(0, s, add_to(1), 0)
    for u in range(2):
        pair_s[u * HALF:(u + 1) * HALF, :] = ownf[u, 1 - parity].astype(BF16)
    pair_copy = remote(pair_s, pair_r, pair_sem.at[0], pair_sem.at[1], s, mate)
    pair_copy.start()

    z_turn(1, 1)
    z_turn(3, 0)

    pair_copy.wait_recv()
    factor = jnp.where(parity == 0, INV_ROOT, 1.0).astype(F32)
    for u in range(2):
        rows = slice(u * HALF, (u + 1) * HALF)
        pieces[z, xh, rows, :] = (
            (ownf[u, parity] + pair_r[rows, :].astype(F32)) * factor
        ).astype(BF16)
    piece = pieces.at[z, xh]
    piece_copy = remote(piece, piece, xp_sem.at[0], xp_sem.at[1], s, partner)
    piece_copy.start()

    z_turn(2, 1)
    z_turn(4, 0)
    other = pieces.at[z, 1 - xh]
    remote(other, other, xp_sem.at[0], xp_sem.at[1], s, partner).wait_recv()

    def p_copy(way, k, i):
        origin = (z + 8 - (k - 1)) % 8 if way == 0 else (z + (k - 1)) % 8
        src = pieces.at[origin, i]
        index = (way * 4 + (k - 1)) * 2 + i
        return remote(src, src, p_send.at[index], p_recv.at[index], s, right if way == 0 else left)

    def p_wait(way, k, i):
        origin = (z + 8 - k) % 8 if way == 0 else (z + k) % 8
        dst = pieces.at[origin, i]
        index = (way * 4 + (k - 1)) * 2 + i
        remote(dst, dst, p_send.at[index], p_recv.at[index], s, right).wait_recv()

    for i in range(2):
        p_copy(0, 1, i).start()
        p_copy(1, 1, i).start()
    z_turn(3, 1)

    def p_turn(k):
        for i in (1, 0):
            for way in range(2):
                if hops(way, k, i):
                    p_wait(way, k, i)
                    if k < 4 and hops(way, k + 1, i):
                        p_copy(way, k + 1, i).start()

    p_turn(1)
    z_turn(4, 1)
    for side in range(2):
        for origin in range(8):
            spread(side, origin).start()
    p_turn(2)
    p_turn(3)
    p_turn(4)
    for g in range(KVH):
        cols = slice(g * HD, (g + 1) * HD)
        kout_ref[:, cols] = pieces[2 * (g % 4), g // 4]
        vout_ref[:, cols] = pieces[2 * (g % 4) + 1, g // 4]

    def kv_done(d, carry):
        kv_out(d).wait_send()
        forward(d).wait_send()
        return carry

    lax.fori_loop(1, 8, kv_done, 0)
    to_sibling.wait_send()

    def dkv_done(t, carry):
        dkv_out(t).wait_send()
        return carry

    lax.fori_loop(0, s, dkv_done, 0)
    lax.fori_loop(s + 1, 16, dkv_done, 0)
    pair_copy.wait_send()
    piece_copy.wait_send()
    for u in range(2):
        x_copy(u).wait_send()
    for way in range(2):
        for k in range(1, 5):
            for u in range(2):
                if hops(way, k, u):
                    for e in range(2):
                        z_copy(way, k, e, u).wait_send()
                    p_copy(way, k, u).wait_send()
    for side in range(2):
        for origin in range(8):
            spread(side, origin).wait()


def local(queries, keys, values, grad_attn, segment_ids, q_weight):
    rows, width = queries.shape
    vmem = pl.BlockSpec(memory_space=pltpu.VMEM)
    anywhere = pl.BlockSpec(memory_space=pl.ANY)
    dma = pltpu.SemaphoreType.DMA
    weight = lax.all_gather(q_weight, "row", axis=0, tiled=True)
    wide, key_grad, value_grad = pl.pallas_call(
        attention_kernel,
        out_shape=(
            jax.ShapeDtypeStruct((rows, H * HD), BF16),
            jax.ShapeDtypeStruct((rows, KVH * HD), BF16),
            jax.ShapeDtypeStruct((rows, KVH * HD), BF16),
        ),
        in_specs=[vmem, anywhere, anywhere, vmem, vmem],
        out_specs=(anywhere, vmem, vmem),
        scratch_shapes=[
            pltpu.VMEM((17, 2, HALF, HD), BF16),
            pltpu.VMEM((17, HALF, PER * HALF), F32),
            pltpu.VMEM((17, HALF, PER * HALF), F32),
            pltpu.VMEM((2, PER * HALF, HD), BF16),
            pltpu.VMEM((2, PER * HALF, HD), BF16),
            pltpu.VMEM((2, PER * HALF, HD), F32),
            pltpu.VMEM((8, 8, PER * HALF), F32),
            pltpu.VMEM((16, 2, HALF, HD), BF16),
            pltpu.VMEM((16, 2, HALF, HD), BF16),
            pltpu.VMEM((2, 2, HALF, HD), F32),
            pltpu.VMEM((2 * HALF, HD), BF16),
            pltpu.VMEM((2 * HALF, HD), BF16),
            pltpu.VMEM((2, 8, 2 * HALF, PER * HD), BF16),
            pltpu.VMEM((8, 2, 2 * HALF, HD), BF16),
            dma((4,)), dma((8,)), dma((8,)), dma((8,)), dma((8,)), dma((16,)), dma((16,)), dma((2,)),
            dma((2,)), dma((2,)), dma((2,)), dma((32,)), dma((32,)), dma((16,)), dma((16,)),
            dma((2, 8)),
        ],
        compiler_params=pltpu.CompilerParams(
            collective_id=0, has_side_effects=True, vmem_limit_bytes=40 * 1024 * 1024
        ),
        cost_estimate=pl.CostEstimate(
            flops=2 * 17 * 5 * 128 * 128 * 512, bytes_accessed=200_000_000, transcendentals=17 * 128 * 512
        ),
    )(queries, keys, values, grad_attn, segment_ids.reshape(32, 128))
    input_sum = jnp.dot(wide, weight, preferred_element_type=F32)
    return (input_sum.astype(BF16), key_grad, value_grad)


def solution(mesh):
    placed = (
        P("row", "col"),
        P("row", None),
        P("row", None),
        P("row", "col"),
        P(),
        P("row", "col"),
    )
    return jax.shard_map(
        local,
        mesh=mesh,
        in_specs=placed,
        out_specs=(P("row", "col"), P("row", None), P("row", None)),
        check_vma=False,
    )
```

time: 634 us -> 133 us (0.21)
  waiting for transfers between devices: 396 us -> 0.68 us
  Pallas kernels: 0 us -> 99.7 us
  starting transfers between devices: 87.1 us -> 0.04 us
  local copies, waits for them, and re-layouts: 70.5 us -> 8.24 us
  matrix products: 46.6 us -> 7.69 us
  other arithmetic: 13.1 us -> 0 us
    all_gather x2 -> x1, waiting for transfers between devices: 163 us -> 0.01 us  [local(): weight = lax.all_gather(q_weight, 'row', axis=0, tiled=True)]
    psum x1 -> x0, waiting for transfers between devices: 151 us -> none  [local(): lax.psum(key_wide.astype(jnp.bfloat16), 'col').astype(jnp.float32)]
    pallas_call x0 -> x1, Pallas kernels: none -> 99.7 us  [local(): pl.pallas_call(attention_kernel, out_shape=(jax.ShapeDtypeStruct((rows, H...]
    ppermute x96 -> x0, starting transfers between devices: 87 us -> none  [shifted(): return lax.ppermute(block, axis, route)]
    ppermute x96 -> x0, waiting for transfers between devices: 81.1 us -> none  [shifted(): return lax.ppermute(block, axis, route)]
    gather x33 -> x0, local copies, waits for them, and re-layouts: 64.6 us -> none  [the longest x32 62.7 us: block_mask(): key_segs = jnp.take(segment_ids, key_places)]
    dot_general x113 -> x1, matrix products: 46.6 us -> 7.69 us  [local(): input_sum = jnp.dot(wide, weight, preferred_element_type=F32)]
  transfers between devices with their start and end apart: 99 -> 1, of which waited for: 63 -> 0; matrix products, arithmetic and copies ran while one was open for 18% -> 0% of each run, Pallas kernels for 0% -> 76%
where the time goes in v1:
time: 133 us; the launch traced here: 130 us
  Pallas kernels  99.7 us (75%)
  between operations  14.1 us (11%)
  local copies, waits for them, and re-layouts  8.24 us (6%)
  matrix products  7.69 us (6%)
    pallas_call x1, Pallas kernels, local(): pl.pallas_call(attention_kernel, out_shape=(jax.ShapeDtypeStruct((rows, H...  99.7 us
    unnamed x14, local copies, waits for them, and re-layouts  8.24 us
    dot_general x1, matrix products, local(): input_sum = jnp.dot(wide, weight, preferred_element_type=F32)  7.69 us
  transfers between devices with their start and end apart: 1, of which 0 were waited for; matrix products, arithmetic and copies ran while one was open for 0% of the time, Pallas kernels for 76%

profile of v1, /device:TPU:1, one launch (start us, length us, event | category | flops | bytes accessed | tf_op | source)
XLA Modules:
  0.0 130.4 jit_solution(13719596785189293726)
XLA Ops:
  7.2 0.0 all-gather.2.cloned.1.call-start
  7.2 0.7 all-gather.2.cloned.1.call-update
  7.9 0.0 copy-start
  7.9 1.0 copy-done
  8.9 0.0 copy-start.1
  8.9 1.0 copy-done.1
  10.0 0.0 copy-start.2
  10.0 0.9 copy-done.2
  10.9 0.0 copy-start.3
  10.9 0.9 copy-done.3
  11.9 0.0 copy-start.4
  11.9 0.7 copy-done.4
  12.6 99.7 %shard_map.85 = (bf16[256,8192]{1,0:T(8,128)(2,1)S(1)}, bf16[256,1024]{1,0:T(8,128)(2,1)S(1)}, bf16[256,1024]{1,0:T(8,128)(2,1)S(1)}) custom-call(bf16[256,512]{1,0:T(8,128)(2,1)S(1)} %copy-done.2, bf16[256,1024]{1,0:T(8,128)(2,1)S(1)} %copy-done, bf16[256,1024]{1,0:T(8,128)(2,1)S(1)} %copy-done.1, bf16[256,512]{1,0:T(8,128)(2,1)S(1)} %copy-done.3, ...), custom_call_target="tpu_custom_call" | custom-call | flops 1426063360 | bytes 200000000 | tf_op jit(solution)/shard_map/pallas_call | solution.py:401
  112.3 0.0 copy-start.5
  112.3 2.0 %copy-done.5 = bf16[256,8192]{1,0:T(8,128)(2,1)} copy-done((bf16[256,8192]{1,0:T(8,128)(2,1)}, bf16[256,8192]{1,0:T(8,128)(2,1)S(1)}, u32[]{:S(2)}) %copy-start.5) | copy-done | bytes 4194328
  114.3 0.0 all-gather.2.cloned.1.call-done
  114.3 7.7 %convolution_convert_fusion = bf16[256,512]{1,0:T(8,128)(2,1)} fusion(bf16[256,8192]{1,0:T(8,128)(2,1)} %copy-done.5, bf16[8192,512]{1,0:T(8,128)(2,1)} %all-gather.2.cloned.1.call-done), kind=kOutput, calls=%fused_computation | convolution fusion | flops 2147614720 | bytes 12845056 | tf_op jit(solution)/shard_map/dot_general | solution.py:436
  122.0 0.8 copy.11
  122.8 0.8 copy.12
Async XLA Ops:
  7.2 107.1 %all-gather.2.cloned.1.call-start = ((), (), s32[]{:S(2)}) async-start(), calls=%async_computation | async-start | bytes 8912896 | tf_op jit(solution)/shard_map/all_gather | solution.py:400
  7.9 1.0 copy-start
  8.9 1.0 copy-start.1
  10.0 0.9 copy-start.2
  10.9 0.9 copy-start.3
  11.9 0.7 copy-start.4
  112.3 2.0 %copy-start.5 = (bf16[256,8192]{1,0:T(8,128)(2,1)}, bf16[256,8192]{1,0:T(8,128)(2,1)S(1)}, u32[]{:S(2)}) copy-start(bf16[256,8192]{1,0:T(8,128)(2,1)S(1)} %get-tuple-element.6) | copy-start | bytes 12582916
Sparse Core Ops, SparseCore 0:
  9.9 76.3 all-gather.1

commit v2 on v1

--- a/solution.py
+++ b/solution.py
@@ -35,15 +35,18 @@
 
 
 def attention_kernel(
-    q_ref, k_hbm, v_hbm, g_ref, seg_ref,
-    wide_hbm, kout_ref, vout_ref,
-    kvbuf, sbuf, dpbuf, q4, g4, dq4, stat, pbuf, rbuf, ownf, pair_s, pair_r, dqbuf, pieces,
-    load_sem, kv_send, kv_recv, fw_send, fw_recv, dkv_send, dkv_recv, pair_sem,
-    xq_send, xq_recv, xp_sem, z_send, z_recv, p_send, p_recv, out_sem,
+    q_ref, k_hbm, v_hbm, g_ref, seg_ref, w_hbm,
+    out_ref, kout_ref, vout_ref,
+    kvbuf, sbuf, dpbuf, q4, g4, dq4, stat, pbuf, mbuf, rbuf, ownf, pair_s, pair_r, dqbuf, pieces,
+    wbuf, acc, part_s, part_r,
+    load_sem, kv_send, kv_recv, fw_send, fw_recv, m_send, m_recv, dkv_send, dkv_recv, pair_sem,
+    xp_sem, z_send, z_recv, p_send, p_recv,
+    wl_sem, wx_send, wx_recv, wy_send, wy_recv, wf_send, wf_recv, ws_send, ws_recv, c_send, c_recv,
 ):
     s = lax.axis_index("row")
     j = lax.axis_index("col")
     chip, core = s // 2, s % 2
+    xl, y = chip // 4, chip % 4
     xh, z = j // 8, j % 8
     sibling = s + 1 - 2 * core
     partner = (1 - xh) * 8 + z
@@ -52,6 +55,8 @@
     parity = z % 2
     mate = j + 1 - 2 * parity
     head = j // 2
+    inner = xl != xh
+    outer = xl == xh
 
     def remote(src, dst, ssem, rsem, row, col):
         return pltpu.make_async_remote_copy(
@@ -79,8 +84,9 @@
         return carry
 
     lax.fori_loop(1, 16, greet, 0)
-    for col in (right, left, partner):
-        pl.semaphore_signal(barrier, inc=1, device_id=(s, col), device_id_type=MESH)
+    across = (1 - xl) * 8 + y * 2 + core
+    for row, col in ((s, right), (s, left), (s, partner), (across, partner)):
+        pl.semaphore_signal(barrier, inc=1, device_id=(row, col), device_id_type=MESH)
 
     for u in range(2):
         for h in range(PER):
@@ -104,7 +110,7 @@
 
     for copy in loads:
         copy.wait()
-    pl.semaphore_wait(barrier, 18)
+    pl.semaphore_wait(barrier, 19)
 
     def kv_copy(d, chip_to, row_to):
         src = kvbuf.at[jnp.where(chip_to > chip, s, 16)]
@@ -122,6 +128,78 @@
     to_sibling = remote(own_half, kvbuf.at[s], kv_send.at[0], kv_recv.at[0], sibling, j)
     lax.fori_loop(1, 8, kv_start, 0)
     to_sibling.start()
+
+    slot = 2 * y + core
+    own_weight = pltpu.make_async_copy(w_hbm, wbuf.at[slot, xh], wl_sem.at[0])
+    weight_x = remote(
+        w_hbm, wbuf.at[slot, xh], wx_send.at[0], wx_recv.at[xh], across, xl * 8 + z
+    )
+    weight_on = remote(
+        wbuf.at[slot, 1 - xh], wbuf.at[slot, 1 - xh], wx_send.at[1], wx_recv.at[1 - xh], across, j
+    )
+    weight_x.start()
+    pl.when(outer)(own_weight.start)
+
+    def slot_at(step, which):
+        return 2 * ((y + step) % 4) + which
+
+    def row_at(step):
+        return xl * 8 + ((y + step) % 4) * 2 + core
+
+    def weight_arrived(e):
+        ref = wbuf.at[slot, e]
+        remote(ref, ref, wx_send.at[0], wx_recv.at[e], across, j).wait_recv()
+
+    def y_copy(e, way):
+        ref = wbuf.at[slot, e]
+        index = 2 * e + way
+        return remote(ref, ref, wy_send.at[index], wy_recv.at[index], row_at(3 if way else 1), j)
+
+    def y_wait(e, way):
+        ref = wbuf.at[slot_at(1 if way else 3, core), e]
+        index = 2 * e + way
+        remote(ref, ref, wy_send.at[index], wy_recv.at[index], s, right).wait_recv()
+
+    def f_ref(step, e, way):
+        return wbuf.at[slot_at(step, core), e, pl.ds(way * 256, 256)]
+
+    def f_copy(e, way):
+        ref = f_ref(1 if way else 3, e, way)
+        index = 2 * e + way
+        return remote(ref, ref, wf_send.at[index], wf_recv.at[index], row_at(3 if way else 1), j)
+
+    def f_wait(e, way):
+        ref = f_ref(2, e, way)
+        index = 2 * e + way
+        remote(ref, ref, wf_send.at[index], wf_recv.at[index], s, right).wait_recv()
+
+    def s_copy(e, i, which):
+        if i < 3:
+            ref = wbuf.at[slot_at((0, 3, 1)[i], which), e]
+        else:
+            ref = wbuf.at[slot_at(2, which), e, pl.ds((i - 3) * 256, 256)]
+        index = 5 * e + i
+        return remote(ref, ref, ws_send.at[index], ws_recv.at[index], sibling, j)
+
+    def weight_start(e):
+        y_copy(e, 0).start()
+        y_copy(e, 1).start()
+        s_copy(e, 0, core).start()
+
+    def weight_pass(e):
+        for way in range(2):
+            y_wait(e, way)
+            f_copy(e, way).start()
+            s_copy(e, 1 + way, core).start()
+
+    def weight_last(e):
+        for way in range(2):
+            f_wait(e, way)
+            s_copy(e, 3 + way, core).start()
+
+    def weight_ready(e):
+        for i in range(5):
+            s_copy(e, i, 1 - core).wait_recv()
 
     sub = lax.broadcasted_iota(jnp.int32, (HALF, HALF), 0).astype(F32)
 
@@ -159,6 +237,16 @@
         return carry
 
     lax.fori_loop(1, 8, arrive, 0)
+
+    @pl.when(inner)
+    def _():
+        weight_arrived(xh)
+
+    @pl.when(outer)
+    def _():
+        own_weight.wait()
+
+    weight_start(xh)
     remote(
         kvbuf.at[sibling], kvbuf.at[sibling], kv_send.at[0], kv_recv.at[0], sibling, j
     ).wait_recv()
@@ -173,6 +261,12 @@
         return carry
 
     lax.fori_loop(1, 8, arrive_two, 0)
+
+    @pl.when(inner)
+    def _():
+        weight_arrived(1 - xh)
+        weight_on.start()
+        weight_start(1 - xh)
 
     for u in range(2):
         top = jnp.max(stat[u], axis=0, keepdims=True)
@@ -192,6 +286,12 @@
         return carry
 
     lax.fori_loop(0, 17, pass_two, 0)
+
+    @pl.when(outer)
+    def _():
+        weight_arrived(1 - xh)
+        weight_start(1 - xh)
+
     for u in range(2):
         total = jnp.sum(stat[2 + u], axis=0, keepdims=True)
         inverse = 1.0 / total
@@ -199,6 +299,9 @@
         stat[2 + u, 0:1, :] = inverse
         stat[6 + u, 0:1, :] = delta
         dq4[u] = jnp.zeros((PER * HALF, HD), F32)
+
+    def m_copy(t):
+        return remote(pbuf.at[t], mbuf.at[t], m_send.at[t], m_recv.at[t], sibling, j)
 
     def dkv_out(t):
         return remote(pbuf.at[t], rbuf.at[s], dkv_send.at[t], dkv_recv.at[s], t, j)
@@ -223,90 +326,81 @@
         def _():
             pbuf[t, 0] = key_part.astype(BF16)
             pbuf[t, 1] = value_part.astype(BF16)
-            dkv_out(t).start()
-
-        return carry
-
-    def x_copy(u):
-        rows = pl.ds(u * HALF, HALF)
-        src = dqbuf.at[xh, z, rows]
-        return remote(src, src, xq_send.at[u], xq_recv.at[u], s, partner)
-
-    def x_wait(u):
-        dst = dqbuf.at[1 - xh, z, pl.ds(u * HALF, HALF)]
-        remote(dst, dst, xq_send.at[u], xq_recv.at[u], s, partner).wait_recv()
-
-    def z_copy(way, k, e, u):
+
+            @pl.when(t == sibling)
+            def _():
+                dkv_out(t).start()
+
+            @pl.when((t != sibling) & (t % 2 != core))
+            def _():
+                m_copy(t).start()
+
+        return carry
+
+    def z_copy(way, k, u):
         origin = (z + 8 - (k - 1)) % 8 if way == 0 else (z + (k - 1)) % 8
-        side = xh if e == 0 else 1 - xh
-        src = dqbuf.at[side, origin, pl.ds(u * HALF, HALF)]
-        index = ((way * 4 + (k - 1)) * 2 + e) * 2 + u
+        src = dqbuf.at[origin, pl.ds(u * HALF, HALF)]
+        index = (way * 4 + (k - 1)) * 2 + u
         return remote(src, src, z_send.at[index], z_recv.at[index], s, right if way == 0 else left)
 
-    def z_wait(way, k, e, u):
+    def z_wait(way, k, u):
         origin = (z + 8 - k) % 8 if way == 0 else (z + k) % 8
-        side = xh if e == 0 else 1 - xh
-        dst = dqbuf.at[side, origin, pl.ds(u * HALF, HALF)]
-        index = ((way * 4 + (k - 1)) * 2 + e) * 2 + u
+        dst = dqbuf.at[origin, pl.ds(u * HALF, HALF)]
+        index = (way * 4 + (k - 1)) * 2 + u
         remote(dst, dst, z_send.at[index], z_recv.at[index], s, right).wait_recv()
 
     def hops(way, k, u):
         return k <= 3 or u == way
 
-    def z_turn(k, e):
+    def z_turn(k):
         for u in (1, 0):
             for way in range(2):
                 if hops(way, k, u):
-                    z_wait(way, k, e, u)
+                    z_wait(way, k, u)
                     if k < 4 and hops(way, k + 1, u):
-                        z_copy(way, k + 1, e, u).start()
+                        z_copy(way, k + 1, u).start()
 
     for u, first, last in ((1, s + 1, 17), (0, 0, s + 1)):
         lax.fori_loop(first, last, pass_three, 0)
         for h in range(PER):
-            dqbuf[xh, z, u * HALF:(u + 1) * HALF, h * HD:(h + 1) * HD] = (
+            dqbuf[z, u * HALF:(u + 1) * HALF, h * HD:(h + 1) * HD] = (
                 dq4[u, h * HD:(h + 1) * HD, :] * INV_ROOT
             ).astype(BF16)
-        z_copy(0, 1, 0, u).start()
-        z_copy(1, 1, 0, u).start()
-        x_copy(u).start()
-
-    def spread(side, origin):
-        lanes = pl.ds(pl.multiple_of((side * 8 + origin) * 512, 512), 512)
-        return pltpu.make_async_copy(
-            dqbuf.at[side, origin], wide_hbm.at[:, lanes], out_sem.at[side, origin]
-        )
-
-    z_turn(1, 0)
-    for u in (1, 0):
-        x_wait(u)
-        z_copy(0, 1, 1, u).start()
-        z_copy(1, 1, 1, u).start()
-    z_turn(2, 0)
-
-    def dkv_wait(r, carry):
+        z_copy(0, 1, u).start()
+        z_copy(1, 1, u).start()
+
+    def merge(d, carry):
+        t = 2 * ((chip + d) % 8) + core
+        remote(pbuf.at[t], mbuf.at[t], m_send.at[t], m_recv.at[t], sibling, j).wait_recv()
+        for i in range(2):
+            pbuf[t, i] = (pbuf[t, i].astype(F32) + mbuf[t, i].astype(F32)).astype(BF16)
+        dkv_out(t).start()
+        return carry
+
+    lax.fori_loop(1, 8, merge, 0)
+    z_turn(1)
+    weight_pass(xh)
+    z_turn(2)
+
+    def dkv_take(r):
         remote(rbuf.at[r], rbuf.at[r], dkv_send.at[r], dkv_recv.at[r], s, right).wait_recv()
-        return carry
-
-    lax.fori_loop(0, s, dkv_wait, 0)
-    lax.fori_loop(s + 1, 16, dkv_wait, 0)
-
-    def add_to(u):
-        def add(r, carry):
-            for i in range(2):
-                ownf[u, i] += rbuf[r, i].astype(F32)
-            return carry
-        return add
-
-    lax.fori_loop(s + 1, 16, add_to(0), 0)
-    lax.fori_loop(0, s, add_to(1), 0)
+        u = jnp.where(r > s, 0, 1)
+        for i in range(2):
+            ownf[u, i] += rbuf[r, i].astype(F32)
+
+    def take(d, carry):
+        dkv_take(2 * ((chip + 8 - d) % 8) + core)
+        return carry
+
+    dkv_take(sibling)
+    lax.fori_loop(1, 8, take, 0)
     for u in range(2):
         pair_s[u * HALF:(u + 1) * HALF, :] = ownf[u, 1 - parity].astype(BF16)
     pair_copy = remote(pair_s, pair_r, pair_sem.at[0], pair_sem.at[1], s, mate)
     pair_copy.start()
 
-    z_turn(1, 1)
-    z_turn(3, 0)
+    z_turn(3)
+    weight_pass(1 - xh)
 
     pair_copy.wait_recv()
     factor = jnp.where(parity == 0, INV_ROOT, 1.0).astype(F32)
@@ -319,8 +413,7 @@
     piece_copy = remote(piece, piece, xp_sem.at[0], xp_sem.at[1], s, partner)
     piece_copy.start()
 
-    z_turn(2, 1)
-    z_turn(4, 0)
+    z_turn(4)
     other = pieces.at[z, 1 - xh]
     remote(other, other, xp_sem.at[0], xp_sem.at[1], s, partner).wait_recv()
 
@@ -339,7 +432,6 @@
     for i in range(2):
         p_copy(0, 1, i).start()
         p_copy(1, 1, i).start()
-    z_turn(3, 1)
 
     def p_turn(k):
         for i in (1, 0):
@@ -349,12 +441,31 @@
                     if k < 4 and hops(way, k + 1, i):
                         p_copy(way, k + 1, i).start()
 
+    def product(e, u):
+        rows = pl.ds(u * HALF, HALF)
+        acc[u] = jnp.zeros((HALF, 512), F32)
+
+        def add(zz, carry):
+            acc[u] += dot_nn(dqbuf[zz, rows, :], wbuf[zz, e])
+            return carry
+
+        lax.fori_loop(0, 8, add, 0)
+
+    def c_copy(u):
+        return remote(part_s.at[u], part_r.at[u], c_send.at[u], c_recv.at[u], s, partner)
+
+    weight_last(1 - xh)
+    weight_ready(1 - xh)
+    for u in range(2):
+        product(1 - xh, u)
+        part_s[u] = acc[u].astype(BF16)
+        c_copy(u).start()
     p_turn(1)
-    z_turn(4, 1)
-    for side in range(2):
-        for origin in range(8):
-            spread(side, origin).start()
+    weight_last(xh)
     p_turn(2)
+    weight_ready(xh)
+    for u in range(2):
+        product(xh, u)
     p_turn(3)
     p_turn(4)
     for g in range(KVH):
@@ -362,79 +473,80 @@
         kout_ref[:, cols] = pieces[2 * (g % 4), g // 4]
         vout_ref[:, cols] = pieces[2 * (g % 4) + 1, g // 4]
 
+    for u in range(2):
+        c_copy(u).wait_recv()
+        out_ref[u * HALF:(u + 1) * HALF, :] = (acc[u] + part_r[u].astype(F32)).astype(BF16)
+
     def kv_done(d, carry):
         kv_out(d).wait_send()
         forward(d).wait_send()
+        dkv_out(2 * ((chip + d) % 8) + core).wait_send()
+        m_copy(2 * ((chip + d) % 8) + 1 - core).wait_send()
         return carry
 
     lax.fori_loop(1, 8, kv_done, 0)
     to_sibling.wait_send()
-
-    def dkv_done(t, carry):
-        dkv_out(t).wait_send()
-        return carry
-
-    lax.fori_loop(0, s, dkv_done, 0)
-    lax.fori_loop(s + 1, 16, dkv_done, 0)
+    dkv_out(sibling).wait_send()
     pair_copy.wait_send()
     piece_copy.wait_send()
-    for u in range(2):
-        x_copy(u).wait_send()
+    weight_x.wait_send()
+    pl.when(inner)(weight_on.wait_send)
+    for u in range(2):
+        c_copy(u).wait_send()
+        for way in range(2):
+            y_copy(u, way).wait_send()
+            f_copy(u, way).wait_send()
+        for i in range(5):
+            s_copy(u, i, core).wait_send()
     for way in range(2):
         for k in range(1, 5):
             for u in range(2):
                 if hops(way, k, u):
-                    for e in range(2):
-                        z_copy(way, k, e, u).wait_send()
+                    z_copy(way, k, u).wait_send()
                     p_copy(way, k, u).wait_send()
-    for side in range(2):
-        for origin in range(8):
-            spread(side, origin).wait()
 
 
 def local(queries, keys, values, grad_attn, segment_ids, q_weight):
     rows, width = queries.shape
     vmem = pl.BlockSpec(memory_space=pltpu.VMEM)
-    anywhere = pl.BlockSpec(memory_space=pl.ANY)
+    anywhere = pl.BlockSpec(memory_space=pltpu.HBM)
     dma = pltpu.SemaphoreType.DMA
-    weight = lax.all_gather(q_weight, "row", axis=0, tiled=True)
-    wide, key_grad, value_grad = pl.pallas_call(
+    scratch = [
+        pltpu.VMEM((17, 2, HALF, HD), BF16),
+        pltpu.VMEM((17, HALF, PER * HALF), F32),
+        pltpu.VMEM((17, HALF, PER * HALF), F32),
+        pltpu.VMEM((2, PER * HALF, HD), BF16),
+        pltpu.VMEM((2, PER * HALF, HD), BF16),
+        pltpu.VMEM((2, PER * HALF, HD), F32),
+        pltpu.VMEM((8, 8, PER * HALF), F32),
+        pltpu.VMEM((16, 2, HALF, HD), BF16),
+        pltpu.VMEM((16, 2, HALF, HD), BF16),
+        pltpu.VMEM((16, 2, HALF, HD), BF16),
+        pltpu.VMEM((2, 2, HALF, HD), F32),
+        pltpu.VMEM((2 * HALF, HD), BF16),
+        pltpu.VMEM((2 * HALF, HD), BF16),
+        pltpu.VMEM((8, 2 * HALF, PER * HD), BF16),
+        pltpu.VMEM((8, 2, 2 * HALF, HD), BF16),
+        pltpu.VMEM((8, 2, 512, 512), BF16),
+        pltpu.VMEM((2, HALF, 512), F32),
+        pltpu.VMEM((2, HALF, 512), BF16),
+        pltpu.VMEM((2, HALF, 512), BF16),
+    ]
+    sizes = (4, 8, 8, 8, 8, 16, 16, 16, 16, 2, 2, 16, 16, 16, 16, 1, 2, 2, 4, 4, 4, 4, 10, 10, 2, 2)
+    return pl.pallas_call(
         attention_kernel,
         out_shape=(
-            jax.ShapeDtypeStruct((rows, H * HD), BF16),
+            jax.ShapeDtypeStruct((rows, width), BF16),
             jax.ShapeDtypeStruct((rows, KVH * HD), BF16),
             jax.ShapeDtypeStruct((rows, KVH * HD), BF16),
         ),
-        in_specs=[vmem, anywhere, anywhere, vmem, vmem],
-        out_specs=(anywhere, vmem, vmem),
-        scratch_shapes=[
-            pltpu.VMEM((17, 2, HALF, HD), BF16),
-            pltpu.VMEM((17, HALF, PER * HALF), F32),
-            pltpu.VMEM((17, HALF, PER * HALF), F32),
-            pltpu.VMEM((2, PER * HALF, HD), BF16),
-            pltpu.VMEM((2, PER * HALF, HD), BF16),
-            pltpu.VMEM((2, PER * HALF, HD), F32),
-            pltpu.VMEM((8, 8, PER * HALF), F32),
-            pltpu.VMEM((16, 2, HALF, HD), BF16),
-            pltpu.VMEM((16, 2, HALF, HD), BF16),
-            pltpu.VMEM((2, 2, HALF, HD), F32),
-            pltpu.VMEM((2 * HALF, HD), BF16),
-            pltpu.VMEM((2 * HALF, HD), BF16),
-            pltpu.VMEM((2, 8, 2 * HALF, PER * HD), BF16),
-            pltpu.VMEM((8, 2, 2 * HALF, HD), BF16),
-            dma((4,)), dma((8,)), dma((8,)), dma((8,)), dma((8,)), dma((16,)), dma((16,)), dma((2,)),
-            dma((2,)), dma((2,)), dma((2,)), dma((32,)), dma((32,)), dma((16,)), dma((16,)),
-            dma((2, 8)),
-        ],
+        in_specs=[vmem, anywhere, anywhere, vmem, vmem, anywhere],
+        out_specs=(vmem, vmem, vmem),
+        scratch_shapes=scratch + [dma((size,)) for size in sizes],
         compiler_params=pltpu.CompilerParams(
-            collective_id=0, has_side_effects=True, vmem_limit_bytes=40 * 1024 * 1024
+            collective_id=0, has_side_effects=True, vmem_limit_bytes=48 * 1024 * 1024
         ),
-        cost_estimate=pl.CostEstimate(
-            flops=2 * 17 * 5 * 128 * 128 * 512, bytes_accessed=200_000_000, transcendentals=17 * 128 * 512
-        ),
-    )(queries, keys, values, grad_attn, segment_ids.reshape(32, 128))
-    input_sum = jnp.dot(wide, weight, preferred_element_type=F32)
-    return (input_sum.astype(BF16), key_grad, value_grad)
+    )(queries, keys, values, grad_attn, segment_ids.reshape(32, 128), q_weight)
 
 
 def solution(mesh):

time: 133 us -> 102 us (0.77); the launches traced: 130 us -> 101 us
  between operations: 14.1 us -> 0.65 us
  matrix products: 7.69 us -> 0 us
  Pallas kernels: 99.7 us -> 92.7 us
    dot_general x1 -> x0, matrix products: 7.69 us -> none  [local(): input_sum = jnp.dot(wide, weight, preferred_element_type=F32)]
    pallas_call x1, Pallas kernels: 99.7 us -> 92.7 us  [local(): pl.pallas_call(attention_kernel, out_shape=(jax.ShapeDtypeStruct((rows, w...]
    unnamed x14 -> x15, local copies, waits for them, and re-layouts: 8.24 us -> 8.02 us
  transfers between devices with their start and end apart: 1 -> 0, of which waited for: 0 -> 0; matrix products, arithmetic and copies ran while one was open for 0% -> 0% of each run, Pallas kernels for 76% -> 0%
where the time goes in v2:
time: 102 us; the launch traced here: 101 us
  Pallas kernels  92.7 us (91%)
  local copies, waits for them, and re-layouts  8.02 us (8%)
    pallas_call x1, Pallas kernels, local(): pl.pallas_call(attention_kernel, out_shape=(jax.ShapeDtypeStruct((rows, w...  92.7 us
    unnamed x15, local copies, waits for them, and re-layouts  8.02 us

profile of v2, /device:TPU:1, one launch (start us, length us, event | category | flops | bytes accessed | tf_op | source)
XLA Modules:
  0.0 101.3 jit_solution(9847803027849383459)
XLA Ops:
  0.6 0.0 copy-start
  0.6 1.0 %copy-done = bf16[256,1024]{1,0:T(8,128)(2,1)S(1)} copy-done((bf16[256,1024]{1,0:T(8,128)(2,1)S(1)}, bf16[256,1024]{1,0:T(8,128)(2,1)}, u32[]{:S(2)}) %copy-start) | copy-done | bytes 524312
  1.7 0.0 copy-start.1
  1.7 1.0 %copy-done.1 = bf16[256,1024]{1,0:T(8,128)(2,1)S(1)} copy-done((bf16[256,1024]{1,0:T(8,128)(2,1)S(1)}, bf16[256,1024]{1,0:T(8,128)(2,1)}, u32[]{:S(2)}) %copy-start.1) | copy-done | bytes 524312
  2.7 0.0 copy-start.2
  2.7 1.0 %copy-done.2 = bf16[512,512]{1,0:T(8,128)(2,1)S(1)} copy-done((bf16[512,512]{1,0:T(8,128)(2,1)S(1)}, bf16[512,512]{1,0:T(8,128)(2,1)}, u32[]{:S(2)}) %copy-start.2) | copy-done | bytes 524312
  3.8 0.0 copy-start.3
  3.8 0.9 copy-done.3
  4.7 0.0 copy-start.4
  4.7 0.9 copy-done.4
  5.7 0.0 copy-start.5
  5.7 0.7 copy-done.5
  6.4 92.7 %shard_map.85 = (bf16[256,512]{1,0:T(8,128)(2,1)S(1)}, bf16[256,1024]{1,0:T(8,128)(2,1)S(1)}, bf16[256,1024]{1,0:T(8,128)(2,1)S(1)}) custom-call(bf16[256,512]{1,0:T(8,128)(2,1)S(1)} %copy-done.3, bf16[256,1024]{1,0:T(8,128)(2,1)S(1)} %copy-done, bf16[256,1024]{1,0:T(8,128)(2,1)S(1)} %copy-done.1, bf16[256,512]{1,0:T(8,128)(2,1)S(1)} %copy-done.4, ...), custom_call_target="tpu_custom_call" | custom-call | tf_op jit(solution)/shard_map/pallas_call | solution.py:536
  99.0 0.7 copy.12
  99.8 0.8 copy.13
  100.5 0.8 copy.14
Async XLA Ops:
  0.6 1.0 %copy-start = (bf16[256,1024]{1,0:T(8,128)(2,1)S(1)}, bf16[256,1024]{1,0:T(8,128)(2,1)}, u32[]{:S(2)}) copy-start(bf16[256,1024]{1,0:T(8,128)(2,1)} %k_hbm.1) | copy-start | bytes 1572868
  1.7 1.0 %copy-start.1 = (bf16[256,1024]{1,0:T(8,128)(2,1)S(1)}, bf16[256,1024]{1,0:T(8,128)(2,1)}, u32[]{:S(2)}) copy-start(bf16[256,1024]{1,0:T(8,128)(2,1)} %v_hbm.1) | copy-start | bytes 1572868
  2.7 1.0 %copy-start.2 = (bf16[512,512]{1,0:T(8,128)(2,1)S(1)}, bf16[512,512]{1,0:T(8,128)(2,1)}, u32[]{:S(2)}) copy-start(bf16[512,512]{1,0:T(8,128)(2,1)} %w_hbm.1) | copy-start | bytes 1572868
  3.8 0.9 copy-start.3
  4.7 0.9 copy-start.4
  5.7 0.7 copy-start.5

commit v3 on v2

--- a/solution.py
+++ b/solution.py
@@ -35,11 +35,11 @@
 
 
 def attention_kernel(
-    q_ref, k_hbm, v_hbm, g_ref, seg_ref, w_hbm,
+    q_hbm, k_hbm, v_hbm, g_hbm, seg_hbm, w_hbm,
     out_ref, kout_ref, vout_ref,
     kvbuf, sbuf, dpbuf, q4, g4, dq4, stat, pbuf, mbuf, rbuf, ownf, pair_s, pair_r, dqbuf, pieces,
-    wbuf, acc, part_s, part_r,
-    load_sem, kv_send, kv_recv, fw_send, fw_recv, m_send, m_recv, dkv_send, dkv_recv, pair_sem,
+    wbuf, acc, part_s, part_r, seg_ref,
+    load_sem, q_sem, kv_send, kv_recv, fw_send, fw_recv, m_send, m_recv, dkv_send, dkv_recv, pair_sem,
     xp_sem, z_send, z_recv, p_send, p_recv,
     wl_sem, wx_send, wx_recv, wy_send, wy_recv, wf_send, wf_recv, ws_send, ws_recv, c_send, c_recv,
 ):
@@ -76,6 +76,16 @@
             )
     for copy in loads:
         copy.start()
+    for u in range(2):
+        for h in range(PER):
+            for i, (ref, buf) in enumerate(((q_hbm, q4), (g_hbm, g4))):
+                pltpu.make_async_copy(
+                    ref.at[pl.ds(u * HALF, HALF), pl.ds(h * HD, HD)],
+                    buf.at[u, pl.ds(h * HD, HD)],
+                    q_sem.at[i],
+                ).start()
+    seg_load = pltpu.make_async_copy(seg_hbm, seg_ref, q_sem.at[2])
+    seg_load.start()
 
     barrier = pltpu.get_barrier_semaphore()
 
@@ -88,11 +98,7 @@
     for row, col in ((s, right), (s, left), (s, partner), (across, partner)):
         pl.semaphore_signal(barrier, inc=1, device_id=(row, col), device_id_type=MESH)
 
-    for u in range(2):
-        for h in range(PER):
-            q4[u, h * HD:(h + 1) * HD, :] = q_ref[u * HALF:(u + 1) * HALF, h * HD:(h + 1) * HD]
-            g4[u, h * HD:(h + 1) * HD, :] = g_ref[u * HALF:(u + 1) * HALF, h * HD:(h + 1) * HD]
-
+    seg_load.wait()
     seg = seg_ref[...]
     counts = [jnp.sum((seg < v).astype(F32), keepdims=True) for v in (1, 2, 3)]
     lane = lax.broadcasted_iota(jnp.int32, (1, HALF), 1).astype(F32)
@@ -110,6 +116,8 @@
 
     for copy in loads:
         copy.wait()
+    pltpu.make_async_copy(q4, q4, q_sem.at[0]).wait()
+    pltpu.make_async_copy(g4, g4, q_sem.at[1]).wait()
     pl.semaphore_wait(barrier, 19)
 
     def kv_copy(d, chip_to, row_to):
@@ -131,14 +139,19 @@
 
     slot = 2 * y + core
     own_weight = pltpu.make_async_copy(w_hbm, wbuf.at[slot, xh], wl_sem.at[0])
-    weight_x = remote(
-        w_hbm, wbuf.at[slot, xh], wx_send.at[0], wx_recv.at[xh], across, xl * 8 + z
-    )
-    weight_on = remote(
-        wbuf.at[slot, 1 - xh], wbuf.at[slot, 1 - xh], wx_send.at[1], wx_recv.at[1 - xh], across, j
-    )
-    weight_x.start()
-    pl.when(outer)(own_weight.start)
+
+    def quarter(i):
+        return pl.ds(i * 128, 128)
+
+    def x_copy(i):
+        return remote(
+            w_hbm.at[quarter(i)], wbuf.at[slot, xh, quarter(i)],
+            wx_send.at[i], wx_recv.at[4 * xh + i], across, xl * 8 + z,
+        )
+
+    def on_copy(i):
+        ref = wbuf.at[slot, 1 - xh, quarter(i)]
+        return remote(ref, ref, wx_send.at[4 + i], wx_recv.at[4 * (1 - xh) + i], across, j)
 
     def slot_at(step, which):
         return 2 * ((y + step) % 4) + which
@@ -146,9 +159,9 @@
     def row_at(step):
         return xl * 8 + ((y + step) % 4) * 2 + core
 
-    def weight_arrived(e):
-        ref = wbuf.at[slot, e]
-        remote(ref, ref, wx_send.at[0], wx_recv.at[e], across, j).wait_recv()
+    def x_wait(e, i):
+        ref = wbuf.at[slot, e, quarter(i)]
+        remote(ref, ref, wx_send.at[0], wx_recv.at[4 * e + i], across, j).wait_recv()
 
     def y_copy(e, way):
         ref = wbuf.at[slot, e]
@@ -181,10 +194,33 @@
         index = 5 * e + i
         return remote(ref, ref, ws_send.at[index], ws_recv.at[index], sibling, j)
 
-    def weight_start(e):
-        y_copy(e, 0).start()
-        y_copy(e, 1).start()
-        s_copy(e, 0, core).start()
+    def y_start(e, i, ref):
+        for way in range(2):
+            index = 2 * e + way
+            remote(
+                ref, wbuf.at[slot, e, quarter(i)], wy_send.at[index], wy_recv.at[index],
+                row_at(3 if way else 1), j,
+            ).start()
+
+    for i in range(4):
+        x_copy(i).start()
+
+    @pl.when(outer)
+    def _():
+        own_weight.start()
+        for i in range(4):
+            y_start(xh, i, w_hbm.at[quarter(i)])
+
+    def weight_inner(i):
+        x_wait(1 - xh, i)
+        on_copy(i).start()
+        x_wait(xh, i)
+        y_start(xh, i, wbuf.at[slot, xh, quarter(i)])
+        y_start(1 - xh, i, wbuf.at[slot, 1 - xh, quarter(i)])
+
+    def weight_outer(i):
+        x_wait(1 - xh, i)
+        y_start(1 - xh, i, wbuf.at[slot, 1 - xh, quarter(i)])
 
     def weight_pass(e):
         for way in range(2):
@@ -240,13 +276,9 @@
 
     @pl.when(inner)
     def _():
-        weight_arrived(xh)
-
-    @pl.when(outer)
-    def _():
-        own_weight.wait()
-
-    weight_start(xh)
+        weight_inner(0)
+        weight_inner(1)
+
     remote(
         kvbuf.at[sibling], kvbuf.at[sibling], kv_send.at[0], kv_recv.at[0], sibling, j
     ).wait_recv()
@@ -264,9 +296,8 @@
 
     @pl.when(inner)
     def _():
-        weight_arrived(1 - xh)
-        weight_on.start()
-        weight_start(1 - xh)
+        weight_inner(2)
+        weight_inner(3)
 
     for u in range(2):
         top = jnp.max(stat[u], axis=0, keepdims=True)
@@ -289,8 +320,12 @@
 
     @pl.when(outer)
     def _():
-        weight_arrived(1 - xh)
-        weight_start(1 - xh)
+        own_weight.wait()
+        for i in range(4):
+            weight_outer(i)
+
+    for e in range(2):
+        s_copy(e, 0, core).start()
 
     for u in range(2):
         total = jnp.sum(stat[2 + u], axis=0, keepdims=True)
@@ -378,8 +413,8 @@
         return carry
 
     lax.fori_loop(1, 8, merge, 0)
+    weight_pass(xh)
     z_turn(1)
-    weight_pass(xh)
     z_turn(2)
 
     def dkv_take(r):
@@ -441,12 +476,11 @@
                     if k < 4 and hops(way, k + 1, i):
                         p_copy(way, k + 1, i).start()
 
-    def product(e, u):
-        rows = pl.ds(u * HALF, HALF)
-        acc[u] = jnp.zeros((HALF, 512), F32)
+    def product(e):
+        acc[...] = jnp.zeros((2 * HALF, 512), F32)
 
         def add(zz, carry):
-            acc[u] += dot_nn(dqbuf[zz, rows, :], wbuf[zz, e])
+            acc[...] += dot_nn(dqbuf[zz], wbuf[zz, e])
             return carry
 
         lax.fori_loop(0, 8, add, 0)
@@ -456,16 +490,15 @@
 
     weight_last(1 - xh)
     weight_ready(1 - xh)
-    for u in range(2):
-        product(1 - xh, u)
-        part_s[u] = acc[u].astype(BF16)
+    product(1 - xh)
+    for u in range(2):
+        part_s[u] = acc[u * HALF:(u + 1) * HALF, :].astype(BF16)
         c_copy(u).start()
     p_turn(1)
     weight_last(xh)
     p_turn(2)
     weight_ready(xh)
-    for u in range(2):
-        product(xh, u)
+    product(xh)
     p_turn(3)
     p_turn(4)
     for g in range(KVH):
@@ -475,7 +508,8 @@
 
     for u in range(2):
         c_copy(u).wait_recv()
-        out_ref[u * HALF:(u + 1) * HALF, :] = (acc[u] + part_r[u].astype(F32)).astype(BF16)
+        rows = slice(u * HALF, (u + 1) * HALF)
+        out_ref[rows, :] = (acc[rows, :] + part_r[u].astype(F32)).astype(BF16)
 
     def kv_done(d, carry):
         kv_out(d).wait_send()
@@ -489,8 +523,14 @@
     dkv_out(sibling).wait_send()
     pair_copy.wait_send()
     piece_copy.wait_send()
-    weight_x.wait_send()
-    pl.when(inner)(weight_on.wait_send)
+    for i in range(4):
+        x_copy(i).wait_send()
+
+    @pl.when(inner)
+    def _():
+        for i in range(4):
+            on_copy(i).wait_send()
+
     for u in range(2):
         c_copy(u).wait_send()
         for way in range(2):
@@ -528,11 +568,12 @@
         pltpu.VMEM((8, 2 * HALF, PER * HD), BF16),
         pltpu.VMEM((8, 2, 2 * HALF, HD), BF16),
         pltpu.VMEM((8, 2, 512, 512), BF16),
-        pltpu.VMEM((2, HALF, 512), F32),
+        pltpu.VMEM((2 * HALF, 512), F32),
         pltpu.VMEM((2, HALF, 512), BF16),
         pltpu.VMEM((2, HALF, 512), BF16),
+        pltpu.VMEM((32, 128), jnp.int32),
     ]
-    sizes = (4, 8, 8, 8, 8, 16, 16, 16, 16, 2, 2, 16, 16, 16, 16, 1, 2, 2, 4, 4, 4, 4, 10, 10, 2, 2)
+    sizes = (4, 3, 8, 8, 8, 8, 16, 16, 16, 16, 2, 2, 16, 16, 16, 16, 1, 8, 8, 4, 4, 4, 4, 10, 10, 2, 2)
     return pl.pallas_call(
         attention_kernel,
         out_shape=(
@@ -540,11 +581,11 @@
             jax.ShapeDtypeStruct((rows, KVH * HD), BF16),
             jax.ShapeDtypeStruct((rows, KVH * HD), BF16),
         ),
-        in_specs=[vmem, anywhere, anywhere, vmem, vmem, anywhere],
+        in_specs=[anywhere] * 6,
         out_specs=(vmem, vmem, vmem),
         scratch_shapes=scratch + [dma((size,)) for size in sizes],
         compiler_params=pltpu.CompilerParams(
-            collective_id=0, has_side_effects=True, vmem_limit_bytes=48 * 1024 * 1024
+            collective_id=0, has_side_effects=True, vmem_limit_bytes=63 * 1024 * 1024
         ),
     )(queries, keys, values, grad_attn, segment_ids.reshape(32, 128), q_weight)
 

time: 102 us -> 88.6 us (0.87)
  Pallas kernels: 92.7 us -> 84 us
  local copies, waits for them, and re-layouts: 8.02 us -> 3.75 us
    pallas_call x1, Pallas kernels: 92.7 us -> 84 us  [local(): pl.pallas_call(attention_kernel, out_shape=(jax.ShapeDtypeStruct((rows, w...]
    unnamed x15 -> x7, local copies, waits for them, and re-layouts: 8.02 us -> 3.75 us
where the time goes in v3:
time: 88.6 us; the launch traced here: 88.4 us
  Pallas kernels  84 us (95%)
  local copies, waits for them, and re-layouts  3.75 us (4%)
    pallas_call x1, Pallas kernels, local(): pl.pallas_call(attention_kernel, out_shape=(jax.ShapeDtypeStruct((rows, w...  84 us
    unnamed x7, local copies, waits for them, and re-layouts  3.75 us

profile of v3, /device:TPU:1, one launch (start us, length us, event | category | flops | bytes accessed | tf_op | source)
XLA Modules:
  0.0 88.4 jit_solution(6628537132159399833)
XLA Ops:
  0.6 84.0 %shard_map.85 = (bf16[256,512]{1,0:T(8,128)(2,1)}, bf16[256,1024]{1,0:T(8,128)(2,1)}, bf16[256,1024]{1,0:T(8,128)(2,1)}) custom-call(bf16[256,512]{1,0:T(8,128)(2,1)} %q_hbm.1, bf16[256,1024]{1,0:T(8,128)(2,1)} %k_hbm.1, bf16[256,1024]{1,0:T(8,128)(2,1)} %v_hbm.1, bf16[256,512]{1,0:T(8,128)(2,1)} %g_hbm.1, s32[32,128]{1,0:T(8,128)} %bitcast.1, ...), custom_call_target="tpu_custom_call" | custom-call | tf_op jit(solution)/shard_map/pallas_call | solution.py:577
  84.6 0.0 copy-start.1
  84.6 1.7 %copy.12 = bf16[256,512]{1,0:T(8,128)(2,1)} copy(bf16[256,512]{1,0:T(8,128)(2,1)} %get-tuple-element.6) | data formatting | bytes 524288
  86.4 0.0 copy-done.1
  86.4 0.0 copy-start
  86.4 0.8 copy.13
  87.2 0.4 copy-done
  87.6 0.8 copy.14
Async XLA Ops:
  84.6 1.7 %copy-start.1 = (bf16[256,1024]{1,0:T(8,128)(2,1)S(1)}, bf16[256,1024]{1,0:T(8,128)(2,1)}, u32[]{:S(2)}) copy-start(bf16[256,1024]{1,0:T(8,128)(2,1)} %get-tuple-element.7) | copy-start | bytes 1572868
  86.4 1.2 %copy-start = (bf16[256,1024]{1,0:T(8,128)(2,1)S(1)}, bf16[256,1024]{1,0:T(8,128)(2,1)}, u32[]{:S(2)}) copy-start(bf16[256,1024]{1,0:T(8,128)(2,1)} %get-tuple-element.8) | copy-start | bytes 1572868

commit v4 on v3

--- a/solution.py
+++ b/solution.py
@@ -15,6 +15,14 @@
 HALF = 128
 PER = 4
 NEG = -1e30
+PLAN = (
+    ("x0", "x1", "x2", "x3",),
+    ("a",),
+    (),
+    ("i0", "i1",),
+    ("i2",),
+    ("m", "z1", "i3", "o", "b", "Wa", "z2", "d", "z3", "q", "Wb", "z4", "px", "La", "p1", "R1b", "P1b", "Lb", "p2", "R1a", "P1a", "R2a", "P2a", "p3", "R2b", "P2b", "p4",),
+)
 MESH = pl.DeviceIdType.MESH
 INV_ROOT = 1.0 / math.sqrt(HD)
 SCALE2 = INV_ROOT * math.log2(math.e)
@@ -202,25 +210,48 @@
                 row_at(3 if way else 1), j,
             ).start()
 
+    steps = {}
+
+    def run(stage):
+        for name in PLAN[stage]:
+            steps[name]()
+
+    def send_own():
+        @pl.when(outer)
+        def _():
+            own_weight.start()
+            for i in range(4):
+                y_start(xh, i, w_hbm.at[quarter(i)])
+
+    def weight_inner(i):
+        @pl.when(inner)
+        def _():
+            x_wait(1 - xh, i)
+            on_copy(i).start()
+            x_wait(xh, i)
+            y_start(xh, i, wbuf.at[slot, xh, quarter(i)])
+            if i == 3:
+                s_copy(xh, 0, core).start()
+
+    def weight_outer():
+        @pl.when(outer)
+        def _():
+            own_weight.wait()
+            s_copy(xh, 0, core).start()
+            for i in range(4):
+                x_wait(1 - xh, i)
+
+    def send_other():
+        y_copy(1 - xh, 0).start()
+        y_copy(1 - xh, 1).start()
+        s_copy(1 - xh, 0, core).start()
+
     for i in range(4):
-        x_copy(i).start()
-
-    @pl.when(outer)
-    def _():
-        own_weight.start()
-        for i in range(4):
-            y_start(xh, i, w_hbm.at[quarter(i)])
-
-    def weight_inner(i):
-        x_wait(1 - xh, i)
-        on_copy(i).start()
-        x_wait(xh, i)
-        y_start(xh, i, wbuf.at[slot, xh, quarter(i)])
-        y_start(1 - xh, i, wbuf.at[slot, 1 - xh, quarter(i)])
-
-    def weight_outer(i):
-        x_wait(1 - xh, i)
-        y_start(1 - xh, i, wbuf.at[slot, 1 - xh, quarter(i)])
+        steps["x%d" % i] = x_copy(i).start
+        steps["i%d" % i] = functools.partial(weight_inner, i)
+    steps["a"] = send_own
+    steps["o"] = weight_outer
+    steps["b"] = send_other
 
     def weight_pass(e):
         for way in range(2):
@@ -233,9 +264,16 @@
             f_wait(e, way)
             s_copy(e, 3 + way, core).start()
 
-    def weight_ready(e):
-        for i in range(5):
+    def weight_ready(e, first, last):
+        for i in range(first, last):
             s_copy(e, i, 1 - core).wait_recv()
+
+    for name, e in (("a", xh), ("b", 1 - xh)):
+        steps["W" + name] = functools.partial(weight_pass, e)
+        steps["L" + name] = functools.partial(weight_last, e)
+        steps["R1" + name] = functools.partial(weight_ready, e, 0, 3)
+        steps["R2" + name] = functools.partial(weight_ready, e, 3, 5)
+    run(0)
 
     sub = lax.broadcasted_iota(jnp.int32, (HALF, HALF), 0).astype(F32)
 
@@ -274,11 +312,7 @@
 
     lax.fori_loop(1, 8, arrive, 0)
 
-    @pl.when(inner)
-    def _():
-        weight_inner(0)
-        weight_inner(1)
-
+    run(1)
     remote(
         kvbuf.at[sibling], kvbuf.at[sibling], kv_send.at[0], kv_recv.at[0], sibling, j
     ).wait_recv()
@@ -294,10 +328,7 @@
 
     lax.fori_loop(1, 8, arrive_two, 0)
 
-    @pl.when(inner)
-    def _():
-        weight_inner(2)
-        weight_inner(3)
+    run(2)
 
     for u in range(2):
         top = jnp.max(stat[u], axis=0, keepdims=True)
@@ -318,15 +349,7 @@
 
     lax.fori_loop(0, 17, pass_two, 0)
 
-    @pl.when(outer)
-    def _():
-        own_weight.wait()
-        for i in range(4):
-            weight_outer(i)
-
-    for e in range(2):
-        s_copy(e, 0, core).start()
-
+    run(3)
     for u in range(2):
         total = jnp.sum(stat[2 + u], axis=0, keepdims=True)
         inverse = 1.0 / total
@@ -403,6 +426,8 @@
             ).astype(BF16)
         z_copy(0, 1, u).start()
         z_copy(1, 1, u).start()
+        if u == 1:
+            run(4)
 
     def merge(d, carry):
         t = 2 * ((chip + d) % 8) + core
@@ -412,10 +437,9 @@
         dkv_out(t).start()
         return carry
 
-    lax.fori_loop(1, 8, merge, 0)
-    weight_pass(xh)
-    z_turn(1)
-    z_turn(2)
+    steps["m"] = lambda: lax.fori_loop(1, 8, merge, 0)
+    for k in range(1, 5):
+        steps["z%d" % k] = functools.partial(z_turn, k)
 
     def dkv_take(r):
         remote(rbuf.at[r], rbuf.at[r], dkv_send.at[r], dkv_recv.at[r], s, right).wait_recv()
@@ -427,30 +451,26 @@
         dkv_take(2 * ((chip + 8 - d) % 8) + core)
         return carry
 
-    dkv_take(sibling)
-    lax.fori_loop(1, 8, take, 0)
-    for u in range(2):
-        pair_s[u * HALF:(u + 1) * HALF, :] = ownf[u, 1 - parity].astype(BF16)
     pair_copy = remote(pair_s, pair_r, pair_sem.at[0], pair_sem.at[1], s, mate)
-    pair_copy.start()
-
-    z_turn(3)
-    weight_pass(1 - xh)
-
-    pair_copy.wait_recv()
-    factor = jnp.where(parity == 0, INV_ROOT, 1.0).astype(F32)
-    for u in range(2):
-        rows = slice(u * HALF, (u + 1) * HALF)
-        pieces[z, xh, rows, :] = (
-            (ownf[u, parity] + pair_r[rows, :].astype(F32)) * factor
-        ).astype(BF16)
     piece = pieces.at[z, xh]
     piece_copy = remote(piece, piece, xp_sem.at[0], xp_sem.at[1], s, partner)
-    piece_copy.start()
-
-    z_turn(4)
-    other = pieces.at[z, 1 - xh]
-    remote(other, other, xp_sem.at[0], xp_sem.at[1], s, partner).wait_recv()
+
+    def gather_rows():
+        dkv_take(sibling)
+        lax.fori_loop(1, 8, take, 0)
+        for u in range(2):
+            pair_s[u * HALF:(u + 1) * HALF, :] = ownf[u, 1 - parity].astype(BF16)
+        pair_copy.start()
+
+    def make_piece():
+        pair_copy.wait_recv()
+        factor = jnp.where(parity == 0, INV_ROOT, 1.0).astype(F32)
+        for u in range(2):
+            rows = slice(u * HALF, (u + 1) * HALF)
+            pieces[z, xh, rows, :] = (
+                (ownf[u, parity] + pair_r[rows, :].astype(F32)) * factor
+            ).astype(BF16)
+        piece_copy.start()
 
     def p_copy(way, k, i):
         origin = (z + 8 - (k - 1)) % 8 if way == 0 else (z + (k - 1)) % 8
@@ -464,9 +484,12 @@
         index = (way * 4 + (k - 1)) * 2 + i
         remote(dst, dst, p_send.at[index], p_recv.at[index], s, right).wait_recv()
 
-    for i in range(2):
-        p_copy(0, 1, i).start()
-        p_copy(1, 1, i).start()
+    def p_begin():
+        other = pieces.at[z, 1 - xh]
+        remote(other, other, xp_sem.at[0], xp_sem.at[1], s, partner).wait_recv()
+        for i in range(2):
+            p_copy(0, 1, i).start()
+            p_copy(1, 1, i).start()
 
     def p_turn(k):
         for i in (1, 0):
@@ -476,31 +499,37 @@
                     if k < 4 and hops(way, k + 1, i):
                         p_copy(way, k + 1, i).start()
 
-    def product(e):
-        acc[...] = jnp.zeros((2 * HALF, 512), F32)
-
-        def add(zz, carry):
-            acc[...] += dot_nn(dqbuf[zz], wbuf[zz, e])
+    def product(e, i, near):
+        if near:
+            acc[i] = jnp.zeros((2 * HALF, 512), F32)
+
+        def add(n, carry):
+            step = n // 2 + n // 4 if near else 2
+            zz = 2 * ((y + step) % 4) + n % 2
+            acc[i] += dot_nn(dqbuf[zz], wbuf[zz, e])
             return carry
 
-        lax.fori_loop(0, 8, add, 0)
+        lax.fori_loop(0, 6 if near else 2, add, 0)
 
     def c_copy(u):
         return remote(part_s.at[u], part_r.at[u], c_send.at[u], c_recv.at[u], s, partner)
 
-    weight_last(1 - xh)
-    weight_ready(1 - xh)
-    product(1 - xh)
-    for u in range(2):
-        part_s[u] = acc[u * HALF:(u + 1) * HALF, :].astype(BF16)
-        c_copy(u).start()
-    p_turn(1)
-    weight_last(xh)
-    p_turn(2)
-    weight_ready(xh)
-    product(xh)
-    p_turn(3)
-    p_turn(4)
+    def product_other():
+        product(1 - xh, 1, False)
+        for u in range(2):
+            part_s[u] = acc[1, u * HALF:(u + 1) * HALF, :].astype(BF16)
+            c_copy(u).start()
+
+    steps["d"] = gather_rows
+    steps["q"] = make_piece
+    steps["px"] = p_begin
+    for k in range(1, 5):
+        steps["p%d" % k] = functools.partial(p_turn, k)
+    steps["P1a"] = functools.partial(product, xh, 0, True)
+    steps["P2a"] = functools.partial(product, xh, 0, False)
+    steps["P1b"] = functools.partial(product, 1 - xh, 1, True)
+    steps["P2b"] = product_other
+    run(5)
     for g in range(KVH):
         cols = slice(g * HD, (g + 1) * HD)
         kout_ref[:, cols] = pieces[2 * (g % 4), g // 4]
@@ -509,7 +538,7 @@
     for u in range(2):
         c_copy(u).wait_recv()
         rows = slice(u * HALF, (u + 1) * HALF)
-        out_ref[rows, :] = (acc[rows, :] + part_r[u].astype(F32)).astype(BF16)
+        out_ref[rows, :] = (acc[0, rows, :] + part_r[u].astype(F32)).astype(BF16)
 
     def kv_done(d, carry):
         kv_out(d).wait_send()
@@ -568,7 +597,7 @@
         pltpu.VMEM((8, 2 * HALF, PER * HD), BF16),
         pltpu.VMEM((8, 2, 2 * HALF, HD), BF16),
         pltpu.VMEM((8, 2, 512, 512), BF16),
-        pltpu.VMEM((2 * HALF, 512), F32),
+        pltpu.VMEM((2, 2 * HALF, 512), F32),
         pltpu.VMEM((2, HALF, 512), BF16),
         pltpu.VMEM((2, HALF, 512), BF16),
         pltpu.VMEM((32, 128), jnp.int32),

time: 88.6 us -> 83 us (0.937)
  the two profiles are of different devices: /device:TPU:1 before, /device:TPU:2 now
where the time goes in v4:
time: 83 us; the launch traced here: 82.8 us
  Pallas kernels  78.4 us (94%)
  local copies, waits for them, and re-layouts  3.75 us (5%)
    pallas_call x1, Pallas kernels, local(): pl.pallas_call(attention_kernel, out_shape=(jax.ShapeDtypeStruct((rows, w...  78.4 us
    unnamed x7, local copies, waits for them, and re-layouts  3.75 us

profile of v4, /device:TPU:2, one launch (start us, length us, event | category | flops | bytes accessed | tf_op | source)
XLA Modules:
  0.0 82.8 jit_solution(1878608518294244745)
XLA Ops:
  0.6 78.4 %shard_map.85 = (bf16[256,512]{1,0:T(8,128)(2,1)}, bf16[256,1024]{1,0:T(8,128)(2,1)}, bf16[256,1024]{1,0:T(8,128)(2,1)}) custom-call(bf16[256,512]{1,0:T(8,128)(2,1)} %q_hbm.1, bf16[256,1024]{1,0:T(8,128)(2,1)} %k_hbm.1, bf16[256,1024]{1,0:T(8,128)(2,1)} %v_hbm.1, bf16[256,512]{1,0:T(8,128)(2,1)} %g_hbm.1, s32[32,128]{1,0:T(8,128)} %bitcast.1, ...), custom_call_target="tpu_custom_call" | custom-call | tf_op jit(solution)/shard_map/pallas_call | solution.py:606
  79.0 0.0 copy-start.1
  79.0 1.7 %copy.12 = bf16[256,512]{1,0:T(8,128)(2,1)} copy(bf16[256,512]{1,0:T(8,128)(2,1)} %get-tuple-element.6) | data formatting | bytes 524288
  80.7 0.0 copy-done.1
  80.7 0.0 copy-start
  80.7 0.8 copy.13
  81.5 0.4 copy-done
  82.0 0.8 copy.14
Async XLA Ops:
  79.0 1.7 %copy-start.1 = (bf16[256,1024]{1,0:T(8,128)(2,1)S(1)}, bf16[256,1024]{1,0:T(8,128)(2,1)}, u32[]{:S(2)}) copy-start(bf16[256,1024]{1,0:T(8,128)(2,1)} %get-tuple-element.7) | copy-start | bytes 1572868
  80.7 1.2 %copy-start = (bf16[256,1024]{1,0:T(8,128)(2,1)S(1)}, bf16[256,1024]{1,0:T(8,128)(2,1)}, u32[]{:S(2)}) copy-start(bf16[256,1024]{1,0:T(8,128)(2,1)} %get-tuple-element.8) | copy-start | bytes 1572868

commit v5 on v4

--- a/solution.py
+++ b/solution.py
@@ -16,12 +16,12 @@
 PER = 4
 NEG = -1e30
 PLAN = (
-    ("x0", "x1", "x2", "x3",),
-    ("a",),
-    (),
-    ("i0", "i1",),
+    ("x0",),
+    ("a", "x1", "x2",),
+    ("x3", "i0",),
+    ("i1",),
     ("i2",),
-    ("m", "z1", "i3", "o", "b", "Wa", "z2", "d", "z3", "q", "Wb", "z4", "px", "La", "p1", "R1b", "P1b", "Lb", "p2", "R1a", "P1a", "R2a", "P2a", "p3", "R2b", "P2b", "p4",),
+    ("m", "z1", "i3", "o", "b", "Wa", "z2", "d", "z3", "q", "z4", "px", "Wb", "La", "p1", "R1b", "P1b", "Lb", "p2", "R1a", "P1a", "R2b", "P2b", "R2a", "P2a", "p3", "p4",),
 )
 MESH = pl.DeviceIdType.MESH
 INV_ROOT = 1.0 / math.sqrt(HD)
@@ -44,10 +44,10 @@
 
 def attention_kernel(
     q_hbm, k_hbm, v_hbm, g_hbm, seg_hbm, w_hbm,
-    out_ref, kout_ref, vout_ref,
+    own_hbm, part_hbm, kout_hbm, vout_hbm,
     kvbuf, sbuf, dpbuf, q4, g4, dq4, stat, pbuf, mbuf, rbuf, ownf, pair_s, pair_r, dqbuf, pieces,
     wbuf, acc, part_s, part_r, seg_ref,
-    load_sem, q_sem, kv_send, kv_recv, fw_send, fw_recv, m_send, m_recv, dkv_send, dkv_recv, pair_sem,
+    load_sem, q_sem, out_sem, kv_send, kv_recv, fw_send, fw_recv, m_send, m_recv, dkv_send, dkv_recv, pair_sem,
     xp_sem, z_send, z_recv, p_send, p_recv,
     wl_sem, wx_send, wx_recv, wy_send, wy_recv, wf_send, wf_recv, ws_send, ws_recv, c_send, c_recv,
 ):
@@ -530,15 +530,23 @@
     steps["P1b"] = functools.partial(product, 1 - xh, 1, True)
     steps["P2b"] = product_other
     run(5)
+    stores = []
     for g in range(KVH):
-        cols = slice(g * HD, (g + 1) * HD)
-        kout_ref[:, cols] = pieces[2 * (g % 4), g // 4]
-        vout_ref[:, cols] = pieces[2 * (g % 4) + 1, g // 4]
-
+        lanes = pl.ds(g * HD, HD)
+        for i, ref in enumerate((kout_hbm, vout_hbm)):
+            stores.append(
+                pltpu.make_async_copy(
+                    pieces.at[2 * (g % 4) + i, g // 4], ref.at[:, lanes], out_sem.at[2 * g + i]
+                )
+            )
+    stores.append(pltpu.make_async_copy(acc.at[0], own_hbm, out_sem.at[16]))
+    for u in range(2):
+        stores.append(pltpu.make_async_copy(part_r.at[u], part_hbm.at[u], out_sem.at[17 + u]))
+    for store in stores[:17]:
+        store.start()
     for u in range(2):
         c_copy(u).wait_recv()
-        rows = slice(u * HALF, (u + 1) * HALF)
-        out_ref[rows, :] = (acc[0, rows, :] + part_r[u].astype(F32)).astype(BF16)
+        stores[17 + u].start()
 
     def kv_done(d, carry):
         kv_out(d).wait_send()
@@ -573,11 +581,12 @@
                 if hops(way, k, u):
                     z_copy(way, k, u).wait_send()
                     p_copy(way, k, u).wait_send()
+    for store in stores:
+        store.wait()
 
 
 def local(queries, keys, values, grad_attn, segment_ids, q_weight):
     rows, width = queries.shape
-    vmem = pl.BlockSpec(memory_space=pltpu.VMEM)
     anywhere = pl.BlockSpec(memory_space=pltpu.HBM)
     dma = pltpu.SemaphoreType.DMA
     scratch = [
@@ -602,21 +611,24 @@
         pltpu.VMEM((2, HALF, 512), BF16),
         pltpu.VMEM((32, 128), jnp.int32),
     ]
-    sizes = (4, 3, 8, 8, 8, 8, 16, 16, 16, 16, 2, 2, 16, 16, 16, 16, 1, 8, 8, 4, 4, 4, 4, 10, 10, 2, 2)
-    return pl.pallas_call(
+    sizes = (4, 3, 19, 8, 8, 8, 8, 16, 16, 16, 16, 2, 2, 16, 16, 16, 16, 1, 8, 8, 4, 4, 4, 4, 10, 10, 2, 2)
+    own, part, key_grad, value_grad = pl.pallas_call(
         attention_kernel,
         out_shape=(
-            jax.ShapeDtypeStruct((rows, width), BF16),
+            jax.ShapeDtypeStruct((rows, width), F32),
+            jax.ShapeDtypeStruct((2, rows // 2, width), BF16),
             jax.ShapeDtypeStruct((rows, KVH * HD), BF16),
             jax.ShapeDtypeStruct((rows, KVH * HD), BF16),
         ),
         in_specs=[anywhere] * 6,
-        out_specs=(vmem, vmem, vmem),
+        out_specs=(anywhere,) * 4,
         scratch_shapes=scratch + [dma((size,)) for size in sizes],
         compiler_params=pltpu.CompilerParams(
             collective_id=0, has_side_effects=True, vmem_limit_bytes=63 * 1024 * 1024
         ),
     )(queries, keys, values, grad_attn, segment_ids.reshape(32, 128), q_weight)
+    input_grad = (own + part.reshape(rows, width).astype(F32)).astype(BF16)
+    return (input_grad, key_grad, value_grad)
 
 
 def solution(mesh):

time: 83 us -> 80.5 us (0.970)
  the two profiles are of different devices: /device:TPU:2 before, /device:TPU:6 now
where the time goes in v5:
time: 80.5 us; the launch traced here: 80.2 us
  Pallas kernels  75.6 us (94%)
  local copies, waits for them, and re-layouts  2.03 us (3%)
  other arithmetic  1.94 us (2%)
    pallas_call x1, Pallas kernels, local(): pl.pallas_call(attention_kernel, out_shape=(jax.ShapeDtypeStruct((rows, w...  75.6 us
    unnamed x6, local copies, waits for them, and re-layouts  2.03 us
    convert_element_type x1, other arithmetic, local(): input_grad = (own + part.reshape(rows, width).astype(F32)).astype(BF16)  1.94 us

profile of v5, /device:TPU:6, one launch (start us, length us, event | category | flops | bytes accessed | tf_op | source)
XLA Modules:
  0.0 80.2 jit_solution(8243283652574803662)
XLA Ops:
  0.6 75.6 %shard_map.85 = (f32[256,512]{1,0:T(8,128)}, bf16[2,128,512]{2,1,0:T(8,128)(2,1)}, bf16[256,1024]{1,0:T(8,128)(2,1)}, bf16[256,1024]{1,0:T(8,128)(2,1)}) custom-call(bf16[256,512]{1,0:T(8,128)(2,1)} %q_hbm.1, bf16[256,1024]{1,0:T(8,128)(2,1)} %k_hbm.1, bf16[256,1024]{1,0:T(8,128)(2,1)} %v_hbm.1, bf16[256,512]{1,0:T(8,128)(2,1)} %g_hbm.1, s32[32,128]{1,0:T(8,128)} %bitcast.4, ...), custom_call_target="tpu_custom_call" | custom-call | tf_op jit(solution)/shard_map/pallas_call | solution.py:615
  76.3 0.0 copy-start.1
  76.3 1.9 %fusion = bf16[256,512]{1,0:T(8,128)(2,1)} fusion(f32[256,512]{1,0:T(8,128)} %get-tuple-element.7, bf16[2,128,512]{2,1,0:T(8,128)(2,1)} %get-tuple-element.8), kind=kLoop, calls=%fused_computation.1 | loop fusion | flops 393216 | bytes 1048576 | tf_op jit(solution)/shard_map/convert_element_type | solution.py:630
  78.2 0.0 copy-done.1
  78.2 0.0 copy-start
  78.2 0.8 copy.11
  79.0 0.4 copy-done
  79.4 0.8 copy.12
Async XLA Ops:
  76.3 1.9 %copy-start.1 = (bf16[256,1024]{1,0:T(8,128)(2,1)S(1)}, bf16[256,1024]{1,0:T(8,128)(2,1)}, u32[]{:S(2)}) copy-start(bf16[256,1024]{1,0:T(8,128)(2,1)} %get-tuple-element.15) | copy-start | bytes 1572868
  78.2 1.2 %copy-start = (bf16[256,1024]{1,0:T(8,128)(2,1)S(1)}, bf16[256,1024]{1,0:T(8,128)(2,1)}, u32[]{:S(2)}) copy-start(bf16[256,1024]{1,0:T(8,128)(2,1)} %get-tuple-element.16) | copy-start | bytes 1572868

commit v6 on v5

--- a/solution.py
+++ b/solution.py
@@ -16,12 +16,12 @@
 PER = 4
 NEG = -1e30
 PLAN = (
-    ("x0",),
-    ("a", "x1", "x2",),
+    ("x0", "x1",),
+    ("a", "x2",),
     ("x3", "i0",),
     ("i1",),
-    ("i2",),
-    ("m", "z1", "i3", "o", "b", "Wa", "z2", "d", "z3", "q", "z4", "px", "Wb", "La", "p1", "R1b", "P1b", "Lb", "p2", "R1a", "P1a", "R2b", "P2b", "R2a", "P2a", "p3", "p4",),
+    ("i2", "i3",),
+    ("m", "z1", "o", "b", "Wa", "z2", "d", "z3", "q", "z4", "px", "Wb", "La", "p1", "R1b", "P1b", "Lb", "p2", "R1a", "P1a", "R2b", "P2b", "R2a", "P2a", "p3", "p4",),
 )
 MESH = pl.DeviceIdType.MESH
 INV_ROOT = 1.0 / math.sqrt(HD)

time: 80.5 us -> 79.1 us (0.983)
  the two profiles are of different devices: /device:TPU:6 before, /device:TPU:1 now
where the time goes in v6:
time: 79.1 us; the launch traced here: 78.7 us
  Pallas kernels  74.1 us (94%)
  local copies, waits for them, and re-layouts  2.03 us (3%)
  other arithmetic  1.94 us (2%)
    pallas_call x1, Pallas kernels, local(): pl.pallas_call(attention_kernel, out_shape=(jax.ShapeDtypeStruct((rows, w...  74.1 us
    unnamed x6, local copies, waits for them, and re-layouts  2.03 us
    convert_element_type x1, other arithmetic, local(): input_grad = (own + part.reshape(rows, width).astype(F32)).astype(BF16)  1.94 us

profile of v6, /device:TPU:1, one launch (start us, length us, event | category | flops | bytes accessed | tf_op | source)
XLA Modules:
  0.0 78.7 jit_solution(13630442707413914444)
XLA Ops:
  0.6 74.1 %shard_map.85 = (f32[256,512]{1,0:T(8,128)}, bf16[2,128,512]{2,1,0:T(8,128)(2,1)}, bf16[256,1024]{1,0:T(8,128)(2,1)}, bf16[256,1024]{1,0:T(8,128)(2,1)}) custom-call(bf16[256,512]{1,0:T(8,128)(2,1)} %q_hbm.1, bf16[256,1024]{1,0:T(8,128)(2,1)} %k_hbm.1, bf16[256,1024]{1,0:T(8,128)(2,1)} %v_hbm.1, bf16[256,512]{1,0:T(8,128)(2,1)} %g_hbm.1, s32[32,128]{1,0:T(8,128)} %bitcast.4, ...), custom_call_target="tpu_custom_call" | custom-call | tf_op jit(solution)/shard_map/pallas_call | solution.py:615
  74.8 0.0 copy-start.1
  74.8 1.9 %fusion = bf16[256,512]{1,0:T(8,128)(2,1)} fusion(f32[256,512]{1,0:T(8,128)} %get-tuple-element.7, bf16[2,128,512]{2,1,0:T(8,128)(2,1)} %get-tuple-element.8), kind=kLoop, calls=%fused_computation.1 | loop fusion | flops 393216 | bytes 1048576 | tf_op jit(solution)/shard_map/convert_element_type | solution.py:630
  76.7 0.0 copy-done.1
  76.7 0.0 copy-start
  76.7 0.8 %copy.11 = bf16[256,1024]{1,0:T(8,128)(2,1)} copy(bf16[256,1024]{1,0:T(8,128)(2,1)S(1)} %copy-done.1) | data formatting | bytes 1048576
  77.5 0.4 copy-done
  77.9 0.8 %copy.12 = bf16[256,1024]{1,0:T(8,128)(2,1)} copy(bf16[256,1024]{1,0:T(8,128)(2,1)S(1)} %copy-done) | data formatting | bytes 1048576
Async XLA Ops:
  74.8 1.9 %copy-start.1 = (bf16[256,1024]{1,0:T(8,128)(2,1)S(1)}, bf16[256,1024]{1,0:T(8,128)(2,1)}, u32[]{:S(2)}) copy-start(bf16[256,1024]{1,0:T(8,128)(2,1)} %get-tuple-element.15) | copy-start | bytes 1572868
  76.7 1.2 %copy-start = (bf16[256,1024]{1,0:T(8,128)(2,1)S(1)}, bf16[256,1024]{1,0:T(8,128)(2,1)}, u32[]{:S(2)}) copy-start(bf16[256,1024]{1,0:T(8,128)(2,1)} %get-tuple-element.16) | copy-start | bytes 1572868

commit v7 on v6

--- a/solution.py
+++ b/solution.py
@@ -21,7 +21,7 @@
     ("x3", "i0",),
     ("i1",),
     ("i2", "i3",),
-    ("m", "z1", "o", "b", "Wa", "z2", "d", "z3", "q", "z4", "px", "Wb", "La", "p1", "R1b", "P1b", "Lb", "p2", "R1a", "P1a", "R2b", "P2b", "R2a", "P2a", "p3", "p4",),
+    ("m", "z1", "o", "b", "Wa", "z2", "d", "z3", "q", "z4", "px", "Wb", "La", "p1", "R1b", "P1b", "Lb", "p2", "R2b", "P2b", "p3", "R1a", "P1a", "R2a", "P2a", "p4",),
 )
 MESH = pl.DeviceIdType.MESH
 INV_ROOT = 1.0 / math.sqrt(HD)

time: 79.1 us -> 81 us (1.024)
  Pallas kernels: 74.1 us -> 76.1 us
    pallas_call x1, Pallas kernels: 74.1 us -> 76.1 us  [local(): pl.pallas_call(attention_kernel, out_shape=(jax.ShapeDtypeStruct((rows, w...]
where the time goes in v7:
time: 81 us; the launch traced here: 80.7 us
  Pallas kernels  76.1 us (94%)
  local copies, waits for them, and re-layouts  2.03 us (3%)
  other arithmetic  1.94 us (2%)
    pallas_call x1, Pallas kernels, local(): pl.pallas_call(attention_kernel, out_shape=(jax.ShapeDtypeStruct((rows, w...  76.1 us
    unnamed x6, local copies, waits for them, and re-layouts  2.03 us
    convert_element_type x1, other arithmetic, local(): input_grad = (own + part.reshape(rows, width).astype(F32)).astype(BF16)  1.94 us

profile of v7, /device:TPU:1, one launch (start us, length us, event | category | flops | bytes accessed | tf_op | source)
XLA Modules:
  0.0 80.7 jit_solution(17301390336842191436)
XLA Ops:
  0.6 76.1 %shard_map.85 = (f32[256,512]{1,0:T(8,128)}, bf16[2,128,512]{2,1,0:T(8,128)(2,1)}, bf16[256,1024]{1,0:T(8,128)(2,1)}, bf16[256,1024]{1,0:T(8,128)(2,1)}) custom-call(bf16[256,512]{1,0:T(8,128)(2,1)} %q_hbm.1, bf16[256,1024]{1,0:T(8,128)(2,1)} %k_hbm.1, bf16[256,1024]{1,0:T(8,128)(2,1)} %v_hbm.1, bf16[256,512]{1,0:T(8,128)(2,1)} %g_hbm.1, s32[32,128]{1,0:T(8,128)} %bitcast.4, ...), custom_call_target="tpu_custom_call" | custom-call | tf_op jit(solution)/shard_map/pallas_call | solution.py:615
  76.7 0.0 copy-start.1
  76.8 1.9 %fusion = bf16[256,512]{1,0:T(8,128)(2,1)} fusion(f32[256,512]{1,0:T(8,128)} %get-tuple-element.7, bf16[2,128,512]{2,1,0:T(8,128)(2,1)} %get-tuple-element.8), kind=kLoop, calls=%fused_computation.1 | loop fusion | flops 393216 | bytes 1048576 | tf_op jit(solution)/shard_map/convert_element_type | solution.py:630
  78.7 0.0 copy-done.1
  78.7 0.0 copy-start
  78.7 0.8 copy.11
  79.5 0.4 copy-done
  79.9 0.8 copy.12
Async XLA Ops:
  76.7 1.9 %copy-start.1 = (bf16[256,1024]{1,0:T(8,128)(2,1)S(1)}, bf16[256,1024]{1,0:T(8,128)(2,1)}, u32[]{:S(2)}) copy-start(bf16[256,1024]{1,0:T(8,128)(2,1)} %get-tuple-element.15) | copy-start | bytes 1572868
  78.7 1.2 %copy-start = (bf16[256,1024]{1,0:T(8,128)(2,1)S(1)}, bf16[256,1024]{1,0:T(8,128)(2,1)}, u32[]{:S(2)}) copy-start(bf16[256,1024]{1,0:T(8,128)(2,1)} %get-tuple-element.16) | copy-start | bytes 1572868

commit v8 on v7

--- a/solution.py
+++ b/solution.py
@@ -21,7 +21,7 @@
     ("x3", "i0",),
     ("i1",),
     ("i2", "i3",),
-    ("m", "z1", "o", "b", "Wa", "z2", "d", "z3", "q", "z4", "px", "Wb", "La", "p1", "R1b", "P1b", "Lb", "p2", "R2b", "P2b", "p3", "R1a", "P1a", "R2a", "P2a", "p4",),
+    ("m", "z1", "o", "b", "Wa", "z2", "d", "z3", "q", "z4", "px", "Wb", "p1", "La", "R1b", "P1b", "Lb", "p2", "R1a", "P1a", "R2b", "P2b", "R2a", "P2a", "p3", "p4",),
 )
 MESH = pl.DeviceIdType.MESH
 INV_ROOT = 1.0 / math.sqrt(HD)

time: 81 us -> 79.8 us (0.985)
  Pallas kernels: 76.1 us -> 74.9 us
    pallas_call x1, Pallas kernels: 76.1 us -> 74.9 us  [local(): pl.pallas_call(attention_kernel, out_shape=(jax.ShapeDtypeStruct((rows, w...]
where the time goes in v8:
time: 79.8 us; the launch traced here: 79.6 us
  Pallas kernels  74.9 us (94%)
  local copies, waits for them, and re-layouts  2.03 us (3%)
  other arithmetic  1.94 us (2%)
    pallas_call x1, Pallas kernels, local(): pl.pallas_call(attention_kernel, out_shape=(jax.ShapeDtypeStruct((rows, w...  74.9 us
    unnamed x6, local copies, waits for them, and re-layouts  2.03 us
    convert_element_type x1, other arithmetic, local(): input_grad = (own + part.reshape(rows, width).astype(F32)).astype(BF16)  1.94 us

profile of v8, /device:TPU:1, one launch (start us, length us, event | category | flops | bytes accessed | tf_op | source)
XLA Modules:
  0.0 79.6 jit_solution(16133821554669792827)
XLA Ops:
  0.6 74.9 %shard_map.85 = (f32[256,512]{1,0:T(8,128)}, bf16[2,128,512]{2,1,0:T(8,128)(2,1)}, bf16[256,1024]{1,0:T(8,128)(2,1)}, bf16[256,1024]{1,0:T(8,128)(2,1)}) custom-call(bf16[256,512]{1,0:T(8,128)(2,1)} %q_hbm.1, bf16[256,1024]{1,0:T(8,128)(2,1)} %k_hbm.1, bf16[256,1024]{1,0:T(8,128)(2,1)} %v_hbm.1, bf16[256,512]{1,0:T(8,128)(2,1)} %g_hbm.1, s32[32,128]{1,0:T(8,128)} %bitcast.4, ...), custom_call_target="tpu_custom_call" | custom-call | tf_op jit(solution)/shard_map/pallas_call | solution.py:615
  75.6 0.0 copy-start.1
  75.6 1.9 %fusion = bf16[256,512]{1,0:T(8,128)(2,1)} fusion(f32[256,512]{1,0:T(8,128)} %get-tuple-element.7, bf16[2,128,512]{2,1,0:T(8,128)(2,1)} %get-tuple-element.8), kind=kLoop, calls=%fused_computation.1 | loop fusion | flops 393216 | bytes 1048576 | tf_op jit(solution)/shard_map/convert_element_type | solution.py:630
  77.5 0.0 copy-done.1
  77.5 0.0 copy-start
  77.5 0.8 copy.11
  78.3 0.4 copy-done
  78.8 0.8 copy.12
Async XLA Ops:
  75.6 1.9 %copy-start.1 = (bf16[256,1024]{1,0:T(8,128)(2,1)S(1)}, bf16[256,1024]{1,0:T(8,128)(2,1)}, u32[]{:S(2)}) copy-start(bf16[256,1024]{1,0:T(8,128)(2,1)} %get-tuple-element.15) | copy-start | bytes 1572868
  77.5 1.2 %copy-start = (bf16[256,1024]{1,0:T(8,128)(2,1)S(1)}, bf16[256,1024]{1,0:T(8,128)(2,1)}, u32[]{:S(2)}) copy-start(bf16[256,1024]{1,0:T(8,128)(2,1)} %get-tuple-element.16) | copy-start | bytes 1572868
